TPU v7x, 512 devices: a whole 4x8x8 slice. The times are simulated.
512 devices in a mesh: row: 32 (over x, y), col: 16 (over z, core).
Axes of the slice: x: 4, y: 8, z: 8, core: 2. Of those that a mesh axis runs over, the one named last changes fastest.
Arguments:
- window: float32 [32, 2048, 16, 256], P('row', None, 'col'), may hold values from -7 to 8, as said below
Outputs:
- factored: float32 [32, 2048, 16, 256], P('row', None, 'col')
Inputs may be any that keep to these rules, and one draw needn't show every extreme that they name: `window`: entries above the diagonal are never read. The leading 2 * 128 by 256 block (lower triangle mirrored) is positive definite, with smallest eigenvalue 1 or more.
All inputs are finite; a program needn't handle non-finite values.
Results may differ from a plain program's by a relative error of at most 0.00028.
Values sent between devices are 32-bit elements; how exact they have to be, the bound alone decides.
A program may use at most 64 MiB of HBM per device.

v0:
```python
import jax
import jax.numpy as jnp
from jax import lax
from jax.sharding import PartitionSpec as P

NB = 128


def unmix_cols(gathered, col_count):
    height = gathered.shape[0]
    width = gathered.shape[1]
    return (
        gathered.reshape(height, col_count, width // col_count)
        .transpose(0, 2, 1)
        .reshape(height, width)
    )


def solve_rows(factor, rows_in):
    return jax.scipy.linalg.solve_triangular(factor, rows_in.T, lower=True).T


def body(window):
    blocks = window[0, :, 0, :]
    local_rows = blocks.shape[0]
    local_cols = blocks.shape[1]
    row_count = lax.axis_size("row")
    col_count = lax.axis_size("col")
    row_index = lax.axis_index("row")
    col_index = lax.axis_index("col")
    tile_height = NB // row_count
    tile_width = NB // col_count
    head_rows = local_cols * col_count // row_count
    groups = row_count // col_count
    for panel_step in range(2):
        first_col = panel_step * tile_width
        after_col = first_col + tile_width
        first_row = panel_step * tile_height
        tile_piece = blocks[first_row : first_row + tile_height, first_col:after_col]
        tile_wide = lax.all_gather(tile_piece, "col", axis=1, tiled=True)
        tile_full = lax.all_gather(tile_wide, "row", axis=0, tiled=True)
        tile_full = tile_full.reshape(row_count, tile_height, NB).transpose(1, 0, 2).reshape(NB, NB)
        diag_tile = unmix_cols(tile_full, col_count)
        symmetric = jnp.tril(diag_tile) + jnp.tril(diag_tile, -1).T
        factor = jnp.tril(jnp.linalg.cholesky(symmetric))
        panel_mine = blocks[:, first_col:after_col]
        gathered = lax.all_gather(panel_mine, "col", axis=1, tiled=True)
        solved = solve_rows(factor, unmix_cols(gathered, col_count))
        diag_rows = lax.dynamic_index_in_dim(
            factor.reshape(tile_height, row_count, NB), row_index, 1, False
        )
        panel_rows = jnp.concatenate(
            [jnp.zeros((first_row, NB), jnp.float32), diag_rows, solved[first_row + tile_height :]],
            0,
        )
        own_cols = lax.dynamic_index_in_dim(
            panel_rows.reshape(local_rows, tile_width, col_count), col_index, 2, False
        )
        sending = panel_rows[:head_rows]
        all_rows = lax.all_gather(sending, "row", axis=0, tiled=True)
        picked = lax.dynamic_index_in_dim(
            all_rows.reshape(groups, col_count, head_rows, NB), col_index, 1, False
        )
        col_rows = picked.transpose(1, 0, 2).reshape(local_cols, NB)
        update = jnp.dot(panel_rows, col_rows[after_col:].T, precision=lax.Precision.HIGHEST)
        trailing = blocks[:, after_col:] - update
        blocks = jnp.concatenate([blocks[:, :first_col], own_cols, trailing], 1)
    global_rows = jnp.arange(local_rows)[:, None] * row_count + row_index
    global_cols = jnp.arange(local_cols)[None, :] * col_count + col_index
    lower_mask = global_rows >= global_cols
    result = jnp.where(lower_mask, blocks, 0.0)
    return result[None, :, None, :]


def solution(mesh):
    in_specs = (P("row", None, "col", None),)
    out_specs = P("row", None, "col", None)
    return jax.shard_map(body, mesh=mesh, in_specs=in_specs, out_specs=out_specs, check_vma=False)
```

profile of v0, /device:TPU:1, one launch (start us, length us, event | category | flops | bytes accessed | tf_op | source)
XLA Modules:
  0.0 377.8 jit_solution(15478815313496594066)
XLA Ops:
  6.5 4.6 %copy.51 = f32[1,2048,1,256]{1,3,2,0:T(8,128)S(1)} copy(f32[1,2048,1,256]{3,2,1,0:T(1,128)} %param.4) | data formatting | bytes 4194304 | tf_op args[0]
  11.1 0.6 slice.65
  11.9 24.5 %all-gather = f32[16,8,4]{1,2,0:T(4,128)S(1)} all-gather(f32[1,8,4]{1,2,0:T(4,128)S(1)} %bitcast.136), channel_id=1, replica_groups=mesh['row'=32,'col'=16] {'col'}, dimensions={0}, use_global_device_ids=true | all-gather | bytes 2176 | tf_op jit(solution)/shard_map/all_gather | solution.py:40
  36.6 39.5 %all-gather.1 = f32[32,4,128]{2,1,0:T(4,128)S(1)} all-gather(f32[1,4,128]{2,1,0:T(4,128)S(1)} %bitcast.137), channel_id=1, replica_groups=mesh['row'=32,'col'=16] {'row'}, dimensions={0}, use_global_device_ids=true | all-gather | bytes 67584 | tf_op jit(solution)/shard_map/all_gather | solution.py:41
  76.0 0.2 copy.54
  76.2 0.2 reshape_reshape.6
  76.7 11.7 %cholesky.44 = f32[128,128]{1,0:T(8,128)S(1)} custom-call(f32[128,128]{1,0:T(8,128)S(1)} %fusion.8), custom_call_target="Cholesky" | custom-call | tf_op jit(solution)/shard_map/jit(cholesky)/cholesky | solution.py:45
  88.6 0.7 compare_reduce_fusion.1
  89.3 0.6 select_bitcast_fusion.1
  90.3 9.8 %custom-call.6 = f32[1,128,128]{1,2,0:T(8,128)S(1)} custom-call(f32[1,128,128]{2,1,0:T(8,128)S(1)} %copy.63), custom_call_target="InvertDiagBlocksLowerTriangular" | custom-call | tf_op jit(solution)/shard_map/jit(_solve_triangular)/triangular_solve | solution.py:20
  100.1 1.8 copy.64
  102.0 1.1 convolution_bitcast_fusion.1
  103.0 0.3 slice.66
  103.4 0.7 pad_maximum_fusion
  104.2 81.0 %all-gather.11.cloned.1.call-done = f32[4096,128]{0,1:T(8,128)} async-done(((f32[128,128]{0,1:T(8,128)}), f32[4096,128]{0,1:T(8,128)}) %all-gather.11.cloned.1.call-update) | async-done | bytes 2097168 | tf_op jit(solution)/shard_map/all_gather | solution.py:60
  185.2 2.0 copy.88
  187.2 0.1 constant_dynamic-slice_fusion.2
  187.3 0.1 copy.67
  187.5 1.9 convolution_subtract_fusion
  189.4 1.3 copy-done
  190.7 0.6 slice.70
  191.3 0.2 all-gather.15.cloned.1.call-start
  191.6 0.1 copy.75
  191.7 0.8 slice_bitcast_fusion
  192.5 21.5 %all-gather.2 = f32[16,8,4]{1,2,0:T(4,128)S(1)} all-gather(f32[1,8,4]{1,2,0:T(4,128)S(1)} %bitcast.138), channel_id=1, replica_groups=mesh['row'=32,'col'=16] {'col'}, dimensions={0}, use_global_device_ids=true | all-gather | bytes 2176 | tf_op jit(solution)/shard_map/all_gather | solution.py:40
  214.1 38.2 %all-gather.3 = f32[32,4,128]{2,1,0:T(4,128)S(1)} all-gather(f32[1,4,128]{2,1,0:T(4,128)S(1)} %bitcast.139), channel_id=1, replica_groups=mesh['row'=32,'col'=16] {'row'}, dimensions={0}, use_global_device_ids=true | all-gather | bytes 67584 | tf_op jit(solution)/shard_map/all_gather | solution.py:41
  252.4 0.2 copy.70
  252.5 0.2 reshape_reshape.7
  253.0 11.7 %cholesky.55 = f32[128,128]{1,0:T(8,128)S(1)} custom-call(f32[128,128]{1,0:T(8,128)S(1)} %fusion.6), custom_call_target="Cholesky" | custom-call | tf_op jit(solution)/shard_map/jit(cholesky)/cholesky | solution.py:45
  264.8 0.6 compare_reduce_fusion
  265.4 0.6 select_bitcast_fusion
  266.0 9.8 %custom-call.7 = f32[1,128,128]{1,2,0:T(8,128)S(1)} custom-call(f32[1,128,128]{2,1,0:T(8,128)S(1)} %get-tuple-element.6), custom_call_target="InvertDiagBlocksLowerTriangular" | custom-call | tf_op jit(solution)/shard_map/jit(_solve_triangular)/triangular_solve | solution.py:20
  276.0 1.8 copy.77
  277.8 1.1 convolution_bitcast_fusion
  278.9 0.3 slice.71
  279.2 1.0 concatenate.45
  280.2 0.7 slice.73
  281.0 0.2 fusion.4
  281.3 0.1 copy.78
  281.4 0.6 copy.79
  282.1 0.7 concatenate.43
  282.9 80.3 %all-gather.15.cloned.1.call-done = f32[4096,128]{0,1:T(8,128)} async-done(((f32[128,128]{0,1:T(8,128)}), f32[4096,128]{0,1:T(8,128)}) %all-gather.15.cloned.1.call-update) | async-done | bytes 2097168 | tf_op jit(solution)/shard_map/all_gather | solution.py:60
  363.2 2.1 copy.89
  365.3 0.1 constant_dynamic-slice_fusion
  365.4 0.1 copy.81
  365.6 1.8 fusion
  367.4 0.2 maximum_select_fusion
  367.6 3.6 copy.82
  (53 shorter events, 2.1 us)
Async XLA Ops:
  6.5 93.6 %all-gather.9.cloned.1.call-start = ((), (), s32[]{:S(2)}) async-start(), calls=%async_computation | async-start | bytes 1114112 | tf_op jit(solution)/shard_map/all_gather | solution.py:47
  11.8 173.5 %all-gather.11.cloned.1.call-start = ((), (), s32[]{:S(2)}) async-start(), calls=%async_computation.1 | async-start | bytes 2162688 | tf_op jit(solution)/shard_map/all_gather | solution.py:60
  104.1 171.8 %all-gather.13.cloned.1.call-start = ((), (), s32[]{:S(2)}) async-start(), calls=%async_computation.2 | async-start | bytes 1114112 | tf_op jit(solution)/shard_map/all_gather | solution.py:47
  189.4 1.3 copy-start
  191.3 171.9 %all-gather.15.cloned.1.call-start = ((), (), s32[]{:S(2)}) async-start(), calls=%async_computation.3 | async-start | bytes 2162688 | tf_op jit(solution)/shard_map/all_gather | solution.py:60
  280.2 2.6 copy-start.2
  363.2 2.4 copy-start.1
  363.2 2.5 copy-start.3
Sparse Core Ops, SparseCore 0:
  11.9 47.8 all-gather.8
  104.2 80.9 all-gather.10
  191.4 44.8 all-gather.12
  281.0 82.1 all-gather.14
where the time goes:
time: 380 us; the launch traced here: 378 us
  waiting for transfers between devices  161 us (42%)
  blocking collectives  124 us (33%)
  other arithmetic  47.1 us (12%)
  local copies, waits for them, and re-layouts  25.8 us (7%)
  between operations  13.6 us (4%)
  matrix products  5.78 us (2%)
    all_gather x2, waiting for transfers between devices, body(): all_rows = lax.all_gather(sending, 'row', axis=0, tiled=True)  161 us
    all_gather x2, blocking collectives, body(): tile_full = lax.all_gather(tile_wide, 'row', axis=0, tiled=True)  77.7 us
    all_gather x2, blocking collectives, body(): tile_wide = lax.all_gather(tile_piece, 'col', axis=1, tiled=True)  46 us
    another operation x6, other arithmetic, body(): factor = jnp.tril(jnp.linalg.cholesky(symmetric))  24.9 us
    another operation x4, other arithmetic, solve_rows(): return jax.scipy.linalg.solve_triangular(factor, rows_in.T, lower=True).T  20.8 us
    unnamed x18, local copies, waits for them, and re-layouts  11.1 us
  transfers between devices with their start and end apart: 4, of which 2 were waited for; matrix products, arithmetic and copies ran while one was open for 13% of the time, Pallas kernels for 0%

commit v1 on v0

v1 whole, which is shorter than its diff:
```python
import jax
import jax.numpy as jnp
from jax import lax
from jax.experimental import pallas as pl
from jax.experimental.pallas import tpu as pltpu
from jax.sharding import PartitionSpec as P

MESH = pl.DeviceIdType.MESH
NROW = 32
NCOL = 16
ROWS = 2048
COLS = 256
HEAD = 128
HALF = ((128, 1024), (1152, 896))
HIGH = lax.Precision.HIGHEST


def gather_kernel(
    x_ref, g_ref, a_ref, b_ref,
    xv, gt, g8, abuf, bbuf,
    xsem, osem, c0s, c0r, rs, rr, bs, br, as_, ar, ks, kr,
):
    p = lax.axis_index("row")
    q = lax.axis_index("col")
    z = q // 2
    core = q % 2

    barrier = pltpu.get_barrier_semaphore()

    @pl.loop(1, NCOL)
    def _(d):
        pl.semaphore_signal(barrier, inc=1, device_id=(p, (q + d) % NCOL), device_id_type=MESH)

    @pl.loop(1, NROW)
    def _(d):
        pl.semaphore_signal(barrier, inc=1, device_id=((p + d) % NROW, q), device_id_type=MESH)

    head_in = pltpu.make_async_copy(x_ref.at[pl.ds(0, 256)], xv.at[pl.ds(0, 256)], xsem.at[0])
    rest_in = pltpu.make_async_copy(x_ref.at[pl.ds(256, 3840)], xv.at[pl.ds(256, 3840)], xsem.at[1])
    head_in.start()
    rest_in.start()
    own = pl.ds(pl.multiple_of(q * 16, 16), 16)

    head_in.wait()
    gt[own, 0:HEAD] = xv[pl.ds(0, HEAD, stride=2), :].T[0:16, :]
    pl.semaphore_wait(barrier, NCOL - 1 + NROW - 1)

    def head_copy(d):
        origin = (q + NCOL - d) % NCOL
        rows = pl.ds(pl.multiple_of(origin * 16, 16), 16)
        return own, rows

    def head_send(d):
        block = gt.at[own, pl.ds(0, HEAD)]
        return pltpu.make_async_remote_copy(
            src_ref=block, dst_ref=block, send_sem=c0s.at[d], recv_sem=c0r.at[d],
            device_id=(p, (q + d) % NCOL), device_id_type=MESH)

    def head_recv(d):
        rows = pl.ds(pl.multiple_of(((q + NCOL - d) % NCOL) * 16, 16), 16)
        block = gt.at[rows, pl.ds(0, HEAD)]
        return pltpu.make_async_remote_copy(
            src_ref=block, dst_ref=block, send_sem=c0s.at[d], recv_sem=c0r.at[d],
            device_id=(p, (q + d) % NCOL), device_id_type=MESH)

    @pl.loop(1, NCOL)
    def _(d):
        head_send(d).start()

    rest_in.wait()

    @pl.loop(1, 16)
    def _(b):
        lanes = pl.ds(pl.multiple_of(b * 128, 128), 128)
        gt[own, lanes] = xv[pl.ds(b * 256, 128, stride=2), :].T[0:16, :]

    def piece(dist, half, which):
        rows = ((z + 8 - dist) % 8) * 2 + which
        start, size = HALF[half]
        return gt.at[pl.ds(pl.multiple_of(rows * 16, 16), 16), pl.ds(start, size)]

    def ring_send(direction, step, half):
        dist = step - 1 if direction == 0 else (9 - step) % 8
        slot = step if direction == 0 else 8 - step
        to = (z + 1) % 8 if direction == 0 else (z + 7) % 8
        block = piece(dist, half, core)
        return pltpu.make_async_remote_copy(
            src_ref=block, dst_ref=block, send_sem=rs.at[direction, half, step],
            recv_sem=rr.at[half, slot], device_id=(p, to * 2 + core), device_id_type=MESH)

    def ring_recv(direction, step, half):
        slot = step if direction == 0 else 8 - step
        block = piece(slot, half, core)
        return pltpu.make_async_remote_copy(
            src_ref=block, dst_ref=block, send_sem=rs.at[direction, half, step],
            recv_sem=rr.at[half, slot], device_id=(p, q), device_id_type=MESH)

    def twin_send(slot, half):
        block = piece(slot, half, core)
        return pltpu.make_async_remote_copy(
            src_ref=block, dst_ref=block, send_sem=bs.at[half, slot],
            recv_sem=br.at[half, slot], device_id=(p, z * 2 + 1 - core), device_id_type=MESH)

    def twin_recv(slot, half):
        block = piece(slot, half, 1 - core)
        return pltpu.make_async_remote_copy(
            src_ref=block, dst_ref=block, send_sem=bs.at[half, slot],
            recv_sem=br.at[half, slot], device_id=(p, z * 2 + 1 - core), device_id_type=MESH)

    reach = {(0, 0): 4, (1, 0): 3, (0, 1): 3, (1, 1): 4}
    for half in range(2):
        ring_send(0, 1, half).start()
        ring_send(1, 1, half).start()
    for half in range(2):
        twin_send(0, half).start()

    @pl.loop(1, NCOL)
    def _(d):
        head_recv(d).wait_recv()

    g8[...] = gt[:, 0:HEAD].T[0:8, :]
    mine = pl.ds(pl.multiple_of(p * 8, 8), 8)
    abuf[mine, :] = g8[...]

    def a_send(d):
        return pltpu.make_async_remote_copy(
            src_ref=g8, dst_ref=abuf.at[mine, :], send_sem=as_.at[d], recv_sem=ar.at[d],
            device_id=((p + d) % NROW, q), device_id_type=MESH)

    def a_recv(d):
        rows = pl.ds(pl.multiple_of(((p + NROW - d) % NROW) * 8, 8), 8)
        return pltpu.make_async_remote_copy(
            src_ref=g8, dst_ref=abuf.at[rows, :], send_sem=as_.at[d], recv_sem=ar.at[d],
            device_id=((p + d) % NROW, q), device_id_type=MESH)

    @pl.loop(1, NROW)
    def _(d):
        a_send(d).start()

    def b_send(d, h):
        return pltpu.make_async_remote_copy(
            src_ref=gt.at[:, pl.ds(0, HEAD)], dst_ref=bbuf.at[h], send_sem=ks.at[d],
            recv_sem=kr.at[h], device_id=((p + d) % NROW, q), device_id_type=MESH)

    for h in range(2):
        @pl.when(p == q + 16 * h)
        def _():
            @pl.loop(1, NROW)
            def _(d):
                b_send(d, h).start()
            bbuf[h] = gt[:, 0:HEAD]

    for step in range(1, 5):
        for half in range(2):
            for direction in range(2):
                last = reach[direction, half]
                if step <= last:
                    ring_recv(direction, step, half).wait_recv()
                    if step < last:
                        ring_send(direction, step + 1, half).start()
                    slot = step if direction == 0 else 8 - step
                    twin_send(slot, half).start()

    @pl.loop(1, NROW)
    def _(d):
        a_recv(d).wait_recv()

    a_out = pltpu.make_async_copy(abuf, a_ref, osem.at[0])
    a_out.start()
    for h in range(2):
        @pl.when(p != q + 16 * h)
        def _():
            b_send(1, h).wait_recv()
    b_out = pltpu.make_async_copy(bbuf, b_ref, osem.at[1])
    b_out.start()
    for half in range(2):
        for slot in range(8):
            twin_recv(slot, half).wait_recv()
    g_out = pltpu.make_async_copy(gt, g_ref, osem.at[2])
    g_out.start()

    @pl.loop(1, NCOL)
    def _(d):
        head_send(d).wait_send()

    @pl.loop(1, NROW)
    def _(d):
        a_send(d).wait_send()

    for h in range(2):
        @pl.when(p == q + 16 * h)
        def _():
            @pl.loop(1, NROW)
            def _(d):
                b_send(d, h).wait_send()

    for half in range(2):
        for direction in range(2):
            for step in range(1, reach[direction, half] + 1):
                ring_send(direction, step, half).wait_send()
        for slot in range(8):
            twin_send(slot, half).wait_send()
    a_out.wait()
    b_out.wait()
    g_out.wait()


def gather(x):
    dma = pltpu.SemaphoreType.DMA
    f32 = jnp.float32
    any_spec = pl.BlockSpec(memory_space=pl.ANY)
    return pl.pallas_call(
        gather_kernel,
        out_shape=(
            jax.ShapeDtypeStruct((256, ROWS), f32),
            jax.ShapeDtypeStruct((256, 256), f32),
            jax.ShapeDtypeStruct((2, 256, HEAD), f32),
        ),
        in_specs=[any_spec],
        out_specs=(any_spec, any_spec, any_spec),
        scratch_shapes=[
            pltpu.VMEM((2 * ROWS, 128), f32),
            pltpu.VMEM((256, ROWS), f32),
            pltpu.VMEM((8, 256), f32),
            pltpu.VMEM((256, 256), f32),
            pltpu.VMEM((2, 256, HEAD), f32),
            dma((2,)), dma((3,)),
            dma((NCOL,)), dma((NCOL,)),
            dma((2, 2, 5)), dma((2, 8)),
            dma((2, 8)), dma((2, 8)),
            dma((NROW,)), dma((NROW,)),
            dma((NROW,)), dma((2,)),
        ],
        compiler_params=pltpu.CompilerParams(
            collective_id=0, has_side_effects=True, vmem_limit_bytes=24 << 20),
        name="gather",
    )(x)


def update_kernel(g_ref, w_ref, l_ref, x_ref, o_ref):
    p = lax.axis_index("row")
    q = lax.axis_index("col")
    size = g_ref.shape[1]
    first = pl.program_id(0) * size
    acc = lax.dot_general(
        g_ref[...], w_ref[...], (((0,), (0,)), ((), ())), precision=HIGH,
        preferred_element_type=jnp.float32)
    row = (first + lax.broadcasted_iota(jnp.int32, (size, 128), 0)) * NROW + p
    lane = lax.broadcasted_iota(jnp.int32, (size, 128), 1)
    left = jnp.where(lane < 16, acc[:, :128], x_ref[pl.ds(0, size, stride=2), :] - acc[:, :128])
    right = x_ref[pl.ds(1, size, stride=2), :] - acc[:, 128:]
    o_ref[pl.ds(0, size, stride=2), :] = jnp.where(row >= lane * NCOL + q, left, 0.0)
    o_ref[pl.ds(1, size, stride=2), :] = jnp.where(row >= (lane + 128) * NCOL + q, right, 0.0)

    @pl.when(pl.program_id(0) == 0)
    def _():
        keep = row[0:8] >= lane[0:8] * NCOL + q
        o_ref[pl.ds(0, 8, stride=2), :] = jnp.where(keep, l_ref[...], 0.0)


def update(g, w, l8, x):
    size = 512
    return pl.pallas_call(
        update_kernel,
        grid=(ROWS // size,),
        out_shape=jax.ShapeDtypeStruct((2 * ROWS, 128), jnp.float32),
        in_specs=[
            pl.BlockSpec((256, size), lambda i: (0, i)),
            pl.BlockSpec((256, 256), lambda i: (0, 0)),
            pl.BlockSpec((8, 128), lambda i: (0, 0)),
            pl.BlockSpec((2 * size, 128), lambda i: (i, 0)),
        ],
        out_specs=pl.BlockSpec((2 * size, 128), lambda i: (i, 0)),
        compiler_params=pltpu.CompilerParams(vmem_limit_bytes=24 << 20),
        name="update",
    )(g, w, l8, x)


def body(window):
    x = window.reshape(2 * ROWS, 128)
    p = lax.axis_index("row")
    q = lax.axis_index("col")
    g, a, b = gather(x)
    natural = a.reshape(NROW, 8, NCOL, 16).transpose(1, 0, 3, 2).reshape(256, 256)
    symmetric = jnp.tril(natural) + jnp.tril(natural, -1).T
    factor = jnp.tril(jnp.linalg.cholesky(symmetric))
    inverse = jax.scipy.linalg.solve_triangular(factor, jnp.eye(256, dtype=jnp.float32), lower=True)
    cols = b.reshape(2, NCOL, 16, HEAD).transpose(2, 1, 3, 0).reshape(256, 256)
    t = jnp.dot(inverse, cols, precision=HIGH)
    col_id = jnp.arange(256)[:, None]
    lane = jnp.arange(256)[None, :]
    pick = (col_id == lane * NCOL + q).astype(jnp.float32)
    t = jnp.where(lane < 16, pick, t)
    w = jnp.dot(inverse.T, t, precision=HIGH)
    w = w.reshape(16, NCOL, 256).transpose(1, 0, 2).reshape(256, 256)
    rows8 = lax.dynamic_index_in_dim(factor.reshape(8, NROW, 256), p, 1, False)
    l8 = lax.dynamic_index_in_dim(rows8.reshape(8, 16, NCOL), q, 2, False)
    l8 = jnp.pad(l8, ((0, 0), (0, 112)))
    out = update(g, w, l8, x)
    return out.reshape(1, ROWS, 1, COLS)


def solution(mesh):
    spec = P("row", None, "col", None)
    return jax.shard_map(body, mesh=mesh, in_specs=(spec,), out_specs=spec, check_vma=False)
```

time: 380 us -> 144 us (0.38)
  the two profiles are of different devices: /device:TPU:1 before, /device:TPU:62 now
where the time goes in v1:
time: 144 us; the launch traced here: 143 us
  Pallas kernels  67.8 us (47%)
  other arithmetic  54.1 us (38%)
  local copies, waits for them, and re-layouts  17.4 us (12%)
  matrix products  2.31 us (2%)
  between operations  1.56 us (1%)
    pallas_call x1, Pallas kernels, gather(): pl.pallas_call(gather_kernel, out_shape=(jax.ShapeDtypeStruct((256, ROWS)...  64.3 us
    another operation x6, other arithmetic, body(): factor = jnp.tril(jnp.linalg.cholesky(symmetric))  34.2 us
    another operation x3, other arithmetic, body(): jax.scipy.linalg.solve_triangular(factor, jnp.eye(256, dtype=jnp.float32)...  19.7 us
    reshape x2, local copies, waits for them, and re-layouts, body(): cols = b.reshape(2, NCOL, 16, HEAD).transpose(2, 1, 3, 0).reshape(256, 256)  5.45 us
    unnamed x9, local copies, waits for them, and re-layouts  4.5 us
    another operation x6, local copies, waits for them, and re-layouts  4.02 us
    pallas_call x1, Pallas kernels, update(): pl.pallas_call(update_kernel, grid=(ROWS // size,), out_shape=jax.ShapeDt...  3.58 us

profile of v1, /device:TPU:62, one launch (start us, length us, event | category | flops | bytes accessed | tf_op | source)
XLA Modules:
  0.0 143.3 jit_solution(18131701842949460062)
XLA Ops:
  0.0 0.0 copy-start
  0.0 1.6 %copy-done = f32[1,2048,1,256]{3,2,1,0:T(1,128)S(1)} copy-done((f32[1,2048,1,256]{3,2,1,0:T(1,128)S(1)}, f32[1,2048,1,256]{3,2,1,0:T(1,128)}, u32[]{:S(2)}) %copy-start) | copy-done | bytes 2097176
  1.6 64.3 %gather.4 = (f32[256,2048]{1,0:T(8,128)S(1)}, f32[256,256]{1,0:T(8,128)S(1)}, f32[2,256,128]{2,1,0:T(8,128)S(1)}) custom-call(f32[4096,128]{1,0:T(8,128)S(1)} %bitcast.55), custom_call_target="tpu_custom_call" | custom-call | tf_op jit(solution)/shard_map/gather/pallas_call | solution.py:212
  65.9 0.0 copy-start.2
  65.9 1.3 copy-done.2
  67.2 0.6 reshape.63
  67.8 1.6 %copy.16 = f32[8,32,16,16]{1,0,3,2:T(8,128)S(1)} copy(f32[8,32,16,16]{2,3,0,1:T(8,128)S(1)} %bitcast.59) | data formatting | bytes 524288 | tf_op jit(solution)/shard_map/transpose | solution.py:284
  69.5 0.3 reshape.64
  69.8 0.1 copy.17
  69.9 0.1 copy.19
  70.1 0.1 bitcast_add_fusion.1
  70.2 0.1 copy.20
  70.4 11.7 %cholesky.49 = f32[128,128]{1,0:T(8,128)S(1)} custom-call(f32[128,128]{1,0:T(8,128)S(1)} %cholesky.115), custom_call_target="Cholesky" | custom-call | tf_op jit(solution)/shard_map/jit(cholesky)/cholesky | solution.py:286
  82.1 9.8 %custom-call.15 = f32[1,128,128]{1,2,0:T(8,128)S(1)} custom-call(f32[1,128,128]{2,1,0:T(8,128)S(1)} %get-tuple-element.34), custom_call_target="InvertDiagBlocksLowerTriangular" | custom-call | tf_op jit(solution)/shard_map/jit(cholesky)/cholesky | solution.py:286
  92.0 0.2 constant_dynamic-update-slice_fusion
  92.2 0.3 convolution_subtract_fusion.1
  92.5 11.9 %cholesky.103 = f32[128,128]{1,0:T(8,128)S(1)} custom-call(f32[128,128]{1,0:T(8,128)S(1)} %convolution_subtract_fusion.1), custom_call_target="Cholesky" | custom-call | tf_op jit(solution)/shard_map/jit(cholesky)/cholesky | solution.py:286
  104.4 0.7 compare_reduce_fusion
  106.4 0.1 triangular_solve.78
  106.5 4.1 %while.1 = (s32[]{:T(128)}, f32[256,256]{1,0:T(8,128)S(1)}, s32[2,2]{1,0:T(2,128)S(1)}, f32[2,128,128]{2,1,0:T(8,128)S(1)}, s32[]{:T(128)}) while((s32[]{:T(128)}, f32[256,256]{1,0:T(8,128)S(1)}, s32[2,2]{1,0:T(2,128)S(1)}, f32[2,128,128]{2,1,0:T(8,128)S(1)}, s32[]{:T(128)}) %tuple.24), condition=%wide.while_cond, body=%wide.while_body.sunk | while | flops 2 | bytes 131181 | solution.py:287
  106.5 0.7 fusion.21
  107.2 1.3 bitcast_dynamic-update-slice_fusion.2
  108.5 0.7 fusion.21
  109.2 1.3 bitcast_dynamic-update-slice_fusion.2
  110.6 19.7 %custom-call.16 = f32[2,128,128]{1,2,0:T(8,128)S(1)} custom-call(f32[2,128,128]{2,1,0:T(8,128)S(1)} %get-tuple-element.18), custom_call_target="InvertDiagBlocksLowerTriangular" | custom-call | tf_op jit(solution)/shard_map/jit(_solve_triangular)/triangular_solve | solution.py:287
  130.3 0.3 fusion.4
  130.5 0.3 convolution_subtract_fusion
  130.8 0.3 fusion.7
  131.1 2.9 %copy.21 = f32[2,16,16,128]{1,2,0,3:T(8,128)} copy(f32[2,16,16,128]{3,2,1,0:T(8,128)S(1)} %bitcast.58) | data formatting | bytes 524288 | tf_op jit(solution)/shard_map/reshape | solution.py:288
  134.0 0.0 copy-start.1
  134.0 2.6 %reshape.66 = f32[256,256]{0,1:T(8,128)S(1)} reshape(f32[16,16,128,2]{1,0,3,2:T(8,128)} %bitcast.60) | data formatting | bytes 524288 | tf_op jit(solution)/shard_map/reshape | solution.py:288
  136.6 0.4 convolution_select_fusion
  137.0 0.6 fusion.3
  137.6 0.2 copy.22
  137.8 0.1 reshape.70
  137.9 0.2 dynamic-slice_reduce_fusion
  138.1 0.0 copy-done.1
  138.1 0.0 copy-start.3
  138.1 1.6 %copy-done.3 = f32[256,2048]{1,0:T(8,128)S(1)} copy-done((f32[256,2048]{1,0:T(8,128)S(1)}, f32[256,2048]{1,0:T(8,128)}, u32[]{:S(2)}) %copy-start.3) | copy-done | bytes 2097176
  139.7 3.6 %update.1 = f32[4096,128]{1,0:T(8,128)} custom-call(f32[256,2048]{1,0:T(8,128)S(1)} %copy-done.3, f32[256,256]{1,0:T(8,128)S(1)} %bitcast.57, f32[8,128]{1,0:T(8,128)S(1)} %pad.5.l_ref, f32[4096,128]{1,0:T(8,128)S(1)} %bitcast.56), custom_call_target="tpu_custom_call" | custom-call | tf_op jit(solution)/shard_map/update/pallas_call | solution.py:263
  (18 shorter events, 0.3 us)
Async XLA Ops:
  0.0 1.6 %copy-start = (f32[1,2048,1,256]{3,2,1,0:T(1,128)S(1)}, f32[1,2048,1,256]{3,2,1,0:T(1,128)}, u32[]{:S(2)}) copy-start(f32[1,2048,1,256]{3,2,1,0:T(1,128)} %param.1) | copy-start | bytes 6291460
  65.9 1.3 copy-start.2
  134.0 4.1 %copy-start.1 = (f32[1,2048,1,256]{3,2,1,0:T(1,128)S(1)}, f32[1,2048,1,256]{3,2,1,0:T(1,128)}, u32[]{:S(2)}) copy-start(f32[1,2048,1,256]{3,2,1,0:T(1,128)} %param.1) | copy-start | bytes 6291460
  138.1 1.6 %copy-start.3 = (f32[256,2048]{1,0:T(8,128)S(1)}, f32[256,2048]{1,0:T(8,128)}, u32[]{:S(2)}) copy-start(f32[256,2048]{1,0:T(8,128)} %copy-done.2) | copy-start | bytes 6291460

commit v2 on v1

--- a/solution.py
+++ b/solution.py
@@ -17,8 +17,8 @@
 
 def gather_kernel(
     x_ref, g_ref, a_ref, b_ref,
-    xv, gt, g8, abuf, bbuf,
-    xsem, osem, c0s, c0r, rs, rr, bs, br, as_, ar, ks, kr,
+    xv, gt, g8, b8, abuf, bbuf,
+    xsem, osem, c0s, c0r, rs, rr, bs, br, as_, ar, ks, kr, ts, tr,
 ):
     p = lax.axis_index("row")
     q = lax.axis_index("col")
@@ -35,6 +35,17 @@
     def _(d):
         pl.semaphore_signal(barrier, inc=1, device_id=((p + d) % NROW, q), device_id_type=MESH)
 
+    for half in range(2):
+        @pl.when((q * 2 + half != p) | (p % NCOL != q))
+        def _():
+            pl.semaphore_signal(
+                barrier, inc=1, device_id=(q * 2 + half, p % NCOL), device_id_type=MESH)
+
+        @pl.when((q + 16 * half != p) | (p // 2 != q))
+        def _():
+            pl.semaphore_signal(
+                barrier, inc=1, device_id=(q + 16 * half, p // 2), device_id_type=MESH)
+
     head_in = pltpu.make_async_copy(x_ref.at[pl.ds(0, 256)], xv.at[pl.ds(0, 256)], xsem.at[0])
     rest_in = pltpu.make_async_copy(x_ref.at[pl.ds(256, 3840)], xv.at[pl.ds(256, 3840)], xsem.at[1])
     head_in.start()
@@ -43,12 +54,11 @@
 
     head_in.wait()
     gt[own, 0:HEAD] = xv[pl.ds(0, HEAD, stride=2), :].T[0:16, :]
-    pl.semaphore_wait(barrier, NCOL - 1 + NROW - 1)
-
-    def head_copy(d):
-        origin = (q + NCOL - d) % NCOL
-        rows = pl.ds(pl.multiple_of(origin * 16, 16), 16)
-        return own, rows
+    waits = NCOL - 1 + NROW - 1
+    for half in range(2):
+        waits += jnp.where((q * 2 + half != p) | (p % NCOL != q), 1, 0)
+        waits += jnp.where((q + 16 * half != p) | (p // 2 != q), 1, 0)
+    pl.semaphore_wait(barrier, waits)
 
     def head_send(d):
         block = gt.at[own, pl.ds(0, HEAD)]
@@ -66,6 +76,29 @@
     @pl.loop(1, NCOL)
     def _(d):
         head_send(d).start()
+
+    side = pl.ds(pl.multiple_of((p // NCOL) * HEAD, HEAD), HEAD)
+
+    def scatter_send(half):
+        rows = pl.ds(pl.multiple_of(q * 16 + half * 8, 8), 8)
+        return pltpu.make_async_remote_copy(
+            src_ref=gt.at[rows, pl.ds(0, HEAD)], dst_ref=b8.at[:, side], send_sem=ts.at[half],
+            recv_sem=tr.at[p // NCOL], device_id=(q * 2 + half, p % NCOL), device_id_type=MESH)
+
+    def scatter_recv(h):
+        return pltpu.make_async_remote_copy(
+            src_ref=b8.at[:, pl.ds(h * HEAD, HEAD)], dst_ref=b8.at[:, pl.ds(h * HEAD, HEAD)],
+            send_sem=ts.at[0], recv_sem=tr.at[h], device_id=(q * 2, p % NCOL), device_id_type=MESH)
+
+    for half in range(2):
+        @pl.when((q * 2 + half != p) | (p % NCOL != q))
+        def _():
+            scatter_send(half).start()
+
+        @pl.when((q * 2 + half == p) & (p % NCOL == q))
+        def _():
+            rows = pl.ds(pl.multiple_of(q * 16 + half * 8, 8), 8)
+            b8[:, side] = gt[rows, 0:HEAD]
 
     rest_in.wait()
 
@@ -137,18 +170,26 @@
     def _(d):
         a_send(d).start()
 
-    def b_send(d, h):
-        return pltpu.make_async_remote_copy(
-            src_ref=gt.at[:, pl.ds(0, HEAD)], dst_ref=bbuf.at[h], send_sem=ks.at[d],
-            recv_sem=kr.at[h], device_id=((p + d) % NROW, q), device_id_type=MESH)
-
     for h in range(2):
-        @pl.when(p == q + 16 * h)
-        def _():
-            @pl.loop(1, NROW)
-            def _(d):
-                b_send(d, h).start()
-            bbuf[h] = gt[:, 0:HEAD]
+        @pl.when((q + 16 * h != p) | (p // 2 != q))
+        def _():
+            scatter_recv(h).wait_recv()
+    bbuf[mine, :] = b8[...]
+
+    def b_send(d):
+        return pltpu.make_async_remote_copy(
+            src_ref=b8, dst_ref=bbuf.at[mine, :], send_sem=ks.at[d], recv_sem=kr.at[d],
+            device_id=((p + d) % NROW, q), device_id_type=MESH)
+
+    def b_recv(d):
+        rows = pl.ds(pl.multiple_of(((p + NROW - d) % NROW) * 8, 8), 8)
+        return pltpu.make_async_remote_copy(
+            src_ref=b8, dst_ref=bbuf.at[rows, :], send_sem=ks.at[d], recv_sem=kr.at[d],
+            device_id=((p + d) % NROW, q), device_id_type=MESH)
+
+    @pl.loop(1, NROW)
+    def _(d):
+        b_send(d).start()
 
     for step in range(1, 5):
         for half in range(2):
@@ -167,10 +208,11 @@
 
     a_out = pltpu.make_async_copy(abuf, a_ref, osem.at[0])
     a_out.start()
-    for h in range(2):
-        @pl.when(p != q + 16 * h)
-        def _():
-            b_send(1, h).wait_recv()
+
+    @pl.loop(1, NROW)
+    def _(d):
+        b_recv(d).wait_recv()
+
     b_out = pltpu.make_async_copy(bbuf, b_ref, osem.at[1])
     b_out.start()
     for half in range(2):
@@ -187,12 +229,14 @@
     def _(d):
         a_send(d).wait_send()
 
-    for h in range(2):
-        @pl.when(p == q + 16 * h)
-        def _():
-            @pl.loop(1, NROW)
-            def _(d):
-                b_send(d, h).wait_send()
+    @pl.loop(1, NROW)
+    def _(d):
+        b_send(d).wait_send()
+
+    for half in range(2):
+        @pl.when((q * 2 + half != p) | (p % NCOL != q))
+        def _():
+            scatter_send(half).wait_send()
 
     for half in range(2):
         for direction in range(2):
@@ -208,13 +252,13 @@
 def gather(x):
     dma = pltpu.SemaphoreType.DMA
     f32 = jnp.float32
-    any_spec = pl.BlockSpec(memory_space=pl.ANY)
+    any_spec = pl.BlockSpec(memory_space=pltpu.HBM)
     return pl.pallas_call(
         gather_kernel,
         out_shape=(
             jax.ShapeDtypeStruct((256, ROWS), f32),
             jax.ShapeDtypeStruct((256, 256), f32),
-            jax.ShapeDtypeStruct((2, 256, HEAD), f32),
+            jax.ShapeDtypeStruct((256, 256), f32),
         ),
         in_specs=[any_spec],
         out_specs=(any_spec, any_spec, any_spec),
@@ -222,14 +266,16 @@
             pltpu.VMEM((2 * ROWS, 128), f32),
             pltpu.VMEM((256, ROWS), f32),
             pltpu.VMEM((8, 256), f32),
+            pltpu.VMEM((8, 256), f32),
             pltpu.VMEM((256, 256), f32),
-            pltpu.VMEM((2, 256, HEAD), f32),
+            pltpu.VMEM((256, 256), f32),
             dma((2,)), dma((3,)),
             dma((NCOL,)), dma((NCOL,)),
             dma((2, 2, 5)), dma((2, 8)),
             dma((2, 8)), dma((2, 8)),
             dma((NROW,)), dma((NROW,)),
-            dma((NROW,)), dma((2,)),
+            dma((NROW,)), dma((NROW,)),
+            dma((2,)), dma((2,)),
         ],
         compiler_params=pltpu.CompilerParams(
             collective_id=0, has_side_effects=True, vmem_limit_bytes=24 << 20),
@@ -237,7 +283,111 @@
     )(x)
 
 
-def update_kernel(g_ref, w_ref, l_ref, x_ref, o_ref):
+def mm(a, b, ca=1, cb=0):
+    return lax.dot_general(a, b, (((ca,), (cb,)), ((), ())), precision=HIGH, preferred_element_type=jnp.float32)
+
+def lane_bcast(v, c):
+    return jnp.broadcast_to(v[:, c:c+1], (8, 128))
+
+def sub_bcast(v, r):
+    return jnp.broadcast_to(v[r:r+1, :], (8, 128))
+
+def invert_factor(m):
+    lane = lax.broadcasted_iota(jnp.int32, (8, 128), 1)
+    sub = lax.broadcasted_iota(jnp.int32, (8, 128), 0)
+    m = list(m)
+    out = []
+    for j in range(16):
+        inside = (lane >= 8*j) & (lane < 8*j+8)
+        own = [lane_bcast(m[j], 8*j+k) for k in range(8)]
+        e = {(i, k): sub_bcast(own[k], i) for k in range(8) for i in range(k, 8)}
+        r = []
+        for k in range(8):
+            rk = lax.rsqrt(e[k, k])
+            r.append(rk)
+            for i in range(k+1, 8):
+                e[i, k] = e[i, k] * rk
+            for c in range(k+1, 8):
+                for i in range(c, 8):
+                    e[i, c] = e[i, c] - e[i, k] * e[c, k]
+        row = jnp.where(inside, jnp.where(lane == sub + 8*j, 1.0, 0.0), m[j])
+        final = jnp.zeros((8, 128), jnp.float32)
+        ups = []
+        for k in range(8):
+            u = sub_bcast(row, k) * r[k]
+            ups.append(u)
+            final = jnp.where(sub == k, u, final)
+            if k < 7:
+                l = own[k] * r[k]
+                row = row - l * u
+                for c in range(k+1, 8):
+                    own[c] = own[c] - l * e[c, k]
+        out.append(jnp.where(lane < 8*j+8, final, 0.0))
+        for i in range(j+1, 16):
+            d = [lane_bcast(m[i], 8*j+k) for k in range(8)]
+            acc = jnp.where(inside, 0.0, m[i])
+            for k in range(8):
+                l = d[k] * r[k]
+                acc = acc - l * ups[k]
+                for c in range(k+1, 8):
+                    d[c] = d[c] - l * e[c, k]
+            m[i] = acc
+    return out
+
+
+def one_hot(match):
+    return jnp.where(match, 1.0, 0.0)
+
+
+def factor_kernel(a_ref, b_ref, w_ref, h_ref, sym, z_ref):
+    p = lax.axis_index("row")
+    q = lax.axis_index("col")
+    row = lax.broadcasted_iota(jnp.int32, (256, 256), 0)
+    col = lax.broadcasted_iota(jnp.int32, (256, 256), 1)
+    row_order = one_hot(row == (col % 8) * NROW + col // 8)
+    col_order = one_hot(col == (row % 16) * NCOL + row // 16)
+    rows = mm(row_order, a_ref[...])
+    sym[...] = jnp.where(row >= col, mm(rows, col_order), mm(col_order, rows, 0, 1))
+    pick = one_hot(row[0:8] * NROW + p == col[0:8])
+    h_ref[...] = mm(mm(pick, sym[...]), col_order, 1, 1)
+
+    z1 = invert_factor([sym[8 * i:8 * i + 8, 0:128] for i in range(16)])
+    for i in range(16):
+        z_ref[8 * i:8 * i + 8, 0:128] = z1[i]
+    z1 = z_ref[0:128, 0:128]
+    low = mm(sym[128:256, 0:128], z1, 1, 1)
+    schur = sym[128:256, 128:256] - mm(low, low, 1, 1)
+    carry = mm(low, z1)
+    z2 = invert_factor([schur[8 * i:8 * i + 8] for i in range(16)])
+    for i in range(16):
+        z_ref[128 + 8 * i:136 + 8 * i, 128:256] = z2[i]
+    z_ref[128:256, 0:128] = -mm(z_ref[128:256, 128:256], carry)
+    z_ref[0:128, 128:256] = jnp.zeros((128, 128), jnp.float32)
+
+    z = mm(z_ref[...], col_order, 1, 1)
+    mixed = mm(z, b_ref[...])
+    side = one_hot(col == (row % 128) * 2 + row // 128)
+    t = jnp.where(col < 16, one_hot(row == col * NCOL + q), mm(mixed, side))
+    w_ref[...] = mm(z, t, 0, 0)
+
+
+def factor(a, b):
+    vmem = pl.BlockSpec(memory_space=pltpu.VMEM)
+    return pl.pallas_call(
+        factor_kernel,
+        out_shape=(
+            jax.ShapeDtypeStruct((256, 256), jnp.float32),
+            jax.ShapeDtypeStruct((8, 256), jnp.float32),
+        ),
+        in_specs=[vmem, vmem],
+        out_specs=(vmem, vmem),
+        scratch_shapes=[pltpu.VMEM((256, 256), jnp.float32), pltpu.VMEM((256, 256), jnp.float32)],
+        compiler_params=pltpu.CompilerParams(vmem_limit_bytes=24 << 20),
+        name="factor",
+    )(a, b)
+
+
+def update_kernel(g_ref, w_ref, h_ref, x_ref, o_ref):
     p = lax.axis_index("row")
     q = lax.axis_index("col")
     size = g_ref.shape[1]
@@ -255,10 +405,10 @@
     @pl.when(pl.program_id(0) == 0)
     def _():
         keep = row[0:8] >= lane[0:8] * NCOL + q
-        o_ref[pl.ds(0, 8, stride=2), :] = jnp.where(keep, l_ref[...], 0.0)
-
-
-def update(g, w, l8, x):
+        o_ref[pl.ds(0, 8, stride=2), :] = jnp.where(keep & (lane[0:8] < 16), mm(h_ref[...], w_ref[:, 0:128]), 0.0)
+
+
+def update(g, w, h, x):
     size = 512
     return pl.pallas_call(
         update_kernel,
@@ -267,36 +417,20 @@
         in_specs=[
             pl.BlockSpec((256, size), lambda i: (0, i)),
             pl.BlockSpec((256, 256), lambda i: (0, 0)),
-            pl.BlockSpec((8, 128), lambda i: (0, 0)),
+            pl.BlockSpec((8, 256), lambda i: (0, 0)),
             pl.BlockSpec((2 * size, 128), lambda i: (i, 0)),
         ],
         out_specs=pl.BlockSpec((2 * size, 128), lambda i: (i, 0)),
         compiler_params=pltpu.CompilerParams(vmem_limit_bytes=24 << 20),
         name="update",
-    )(g, w, l8, x)
+    )(g, w, h, x)
 
 
 def body(window):
     x = window.reshape(2 * ROWS, 128)
-    p = lax.axis_index("row")
-    q = lax.axis_index("col")
     g, a, b = gather(x)
-    natural = a.reshape(NROW, 8, NCOL, 16).transpose(1, 0, 3, 2).reshape(256, 256)
-    symmetric = jnp.tril(natural) + jnp.tril(natural, -1).T
-    factor = jnp.tril(jnp.linalg.cholesky(symmetric))
-    inverse = jax.scipy.linalg.solve_triangular(factor, jnp.eye(256, dtype=jnp.float32), lower=True)
-    cols = b.reshape(2, NCOL, 16, HEAD).transpose(2, 1, 3, 0).reshape(256, 256)
-    t = jnp.dot(inverse, cols, precision=HIGH)
-    col_id = jnp.arange(256)[:, None]
-    lane = jnp.arange(256)[None, :]
-    pick = (col_id == lane * NCOL + q).astype(jnp.float32)
-    t = jnp.where(lane < 16, pick, t)
-    w = jnp.dot(inverse.T, t, precision=HIGH)
-    w = w.reshape(16, NCOL, 256).transpose(1, 0, 2).reshape(256, 256)
-    rows8 = lax.dynamic_index_in_dim(factor.reshape(8, NROW, 256), p, 1, False)
-    l8 = lax.dynamic_index_in_dim(rows8.reshape(8, 16, NCOL), q, 2, False)
-    l8 = jnp.pad(l8, ((0, 0), (0, 112)))
-    out = update(g, w, l8, x)
+    w, h = factor(a, b)
+    out = update(g, w, h, x)
     return out.reshape(1, ROWS, 1, COLS)
 
 

time: 144 us -> 58.7 us (0.41)
  the two profiles are of different devices: /device:TPU:62 before, /device:TPU:1 now
where the time goes in v2:
time: 58.7 us; the launch traced here: 58.5 us
  Pallas kernels  56.9 us (97%)
  local copies, waits for them, and re-layouts  1.59 us (3%)
    pallas_call x1, Pallas kernels, gather(): pl.pallas_call(gather_kernel, out_shape=(jax.ShapeDtypeStruct((256, ROWS)...  40.3 us
    pallas_call x1, Pallas kernels, factor(): pl.pallas_call(factor_kernel, out_shape=(jax.ShapeDtypeStruct((256, 256),...  12.8 us
    pallas_call x1, Pallas kernels, update(): pl.pallas_call(update_kernel, grid=(ROWS // size,), out_shape=jax.ShapeDt...  3.76 us
    unnamed x4, local copies, waits for them, and re-layouts  1.59 us

profile of v2, /device:TPU:1, one launch (start us, length us, event | category | flops | bytes accessed | tf_op | source)
XLA Modules:
  0.0 58.5 jit_solution(3132327727148055224)
XLA Ops:
  0.0 0.0 copy-start
  0.0 1.6 %copy-done = f32[1,2048,1,256]{3,2,1,0:T(1,128)S(1)} copy-done((f32[1,2048,1,256]{3,2,1,0:T(1,128)S(1)}, f32[1,2048,1,256]{3,2,1,0:T(1,128)}, u32[]{:S(2)}) %copy-start) | copy-done | bytes 2097176
  1.6 0.0 copy-start.1
  1.6 40.3 %gather.1 = (f32[256,2048]{1,0:T(8,128)S(1)}, f32[256,256]{1,0:T(8,128)S(1)}, f32[256,256]{1,0:T(8,128)S(1)}) custom-call(f32[4096,128]{1,0:T(8,128)S(1)} %bitcast.2), custom_call_target="tpu_custom_call" | custom-call | tf_op jit(solution)/shard_map/gather/pallas_call | solution.py:256
  41.9 12.8 %factor.1 = (f32[256,256]{1,0:T(8,128)S(1)}, f32[8,256]{1,0:T(8,128)S(1)}) custom-call(f32[256,256]{1,0:T(8,128)S(1)} %get-tuple-element.11.a_ref, f32[256,256]{1,0:T(8,128)S(1)} %get-tuple-element.12.b_ref), custom_call_target="tpu_custom_call" | custom-call | tf_op jit(solution)/shard_map/factor/pallas_call | solution.py:376
  54.8 0.0 copy-done.1
  54.8 3.8 %update.1 = f32[4096,128]{1,0:T(8,128)} custom-call(f32[256,2048]{1,0:T(8,128)S(1)} %get-tuple-element.10.g_ref, f32[256,256]{1,0:T(8,128)S(1)} %get-tuple-element.13.w_ref, f32[8,256]{1,0:T(8,128)S(1)} %get-tuple-element.14.h_ref, f32[4096,128]{1,0:T(8,128)S(1)} %bitcast.3), custom_call_target="tpu_custom_call" | custom-call | tf_op jit(solution)/shard_map/update/pallas_call | solution.py:413
Async XLA Ops:
  0.0 1.6 %copy-start = (f32[1,2048,1,256]{3,2,1,0:T(1,128)S(1)}, f32[1,2048,1,256]{3,2,1,0:T(1,128)}, u32[]{:S(2)}) copy-start(f32[1,2048,1,256]{3,2,1,0:T(1,128)} %param.1) | copy-start | bytes 6291460
  1.6 53.2 %copy-start.1 = (f32[1,2048,1,256]{3,2,1,0:T(1,128)S(1)}, f32[1,2048,1,256]{3,2,1,0:T(1,128)}, u32[]{:S(2)}) copy-start(f32[1,2048,1,256]{3,2,1,0:T(1,128)} %param.1) | copy-start | bytes 6291460

commit v3 on v1

v3 whole, which is shorter than its diff:
```python
import jax
import jax.numpy as jnp
from jax import lax
from jax.experimental import pallas as pl
from jax.experimental.pallas import tpu as pltpu
from jax.sharding import PartitionSpec as P

MESH = pl.DeviceIdType.MESH
NROW = 32
NCOL = 16
ROWS = 2048
COLS = 256
HEAD = 128
HALF = ((128, 1024), (1152, 896))
REACH = {(0, 0): 4, (1, 0): 3, (0, 1): 3, (1, 1): 4}
HIGH = lax.Precision.HIGHEST


def mm(a, b, ca=1, cb=0):
    return lax.dot_general(a, b, (((ca,), (cb,)), ((), ())), precision=HIGH, preferred_element_type=jnp.float32)

def lane_bcast(v, c):
    return jnp.broadcast_to(v[:, c:c+1], (8, 128))

def sub_bcast(v, r):
    return jnp.broadcast_to(v[r:r+1, :], (8, 128))

def invert_factor(m):
    lane = lax.broadcasted_iota(jnp.int32, (8, 128), 1)
    sub = lax.broadcasted_iota(jnp.int32, (8, 128), 0)
    m = list(m)
    out = []
    for j in range(16):
        inside = (lane >= 8*j) & (lane < 8*j+8)
        own = [lane_bcast(m[j], 8*j+k) for k in range(8)]
        e = {(i, k): sub_bcast(own[k], i) for k in range(8) for i in range(k, 8)}
        r = []
        for k in range(8):
            rk = lax.rsqrt(e[k, k])
            r.append(rk)
            for i in range(k+1, 8):
                e[i, k] = e[i, k] * rk
            for c in range(k+1, 8):
                for i in range(c, 8):
                    e[i, c] = e[i, c] - e[i, k] * e[c, k]
        row = jnp.where(inside, jnp.where(lane == sub + 8*j, 1.0, 0.0), m[j])
        final = jnp.zeros((8, 128), jnp.float32)
        ups = []
        for k in range(8):
            u = sub_bcast(row, k) * r[k]
            ups.append(u)
            final = jnp.where(sub == k, u, final)
            if k < 7:
                l = own[k] * r[k]
                row = row - l * u
                for c in range(k+1, 8):
                    own[c] = own[c] - l * e[c, k]
        out.append(jnp.where(lane < 8*j+8, final, 0.0))
        for i in range(j+1, 16):
            d = [lane_bcast(m[i], 8*j+k) for k in range(8)]
            acc = jnp.where(inside, 0.0, m[i])
            for k in range(8):
                l = d[k] * r[k]
                acc = acc - l * ups[k]
                for c in range(k+1, 8):
                    d[c] = d[c] - l * e[c, k]
            m[i] = acc
    return out


def parts(v):
    high = v.astype(jnp.bfloat16)
    rest = v - high.astype(jnp.float32)
    middle = rest.astype(jnp.bfloat16)
    return high, middle, (rest - middle.astype(jnp.float32)).astype(jnp.bfloat16)


def one_hot(match):
    return jnp.where(match, 1.0, 0.0).astype(jnp.bfloat16)


def pick_left(chosen, v, ca=1, cb=0):
    return sum(
        lax.dot_general(chosen, part, (((ca,), (cb,)), ((), ())), preferred_element_type=jnp.float32)
        for part in parts(v))


def pick_right(v, chosen, ca=1, cb=0):
    return sum(
        lax.dot_general(part, chosen, (((ca,), (cb,)), ((), ())), preferred_element_type=jnp.float32)
        for part in parts(v))


def panel_kernel(
    x_ref, g_ref, w_ref, h_ref,
    xv, own, head, g8, b8, abuf, bbuf, sym, work, carry, zd, zb,
    xsem, osem, hs, hr, rs, rr, bs, br, as_, ar, ks, kr, ts, tr, us, ur,
):
    p = lax.axis_index("row")
    q = lax.axis_index("col")
    z = q // 2
    core = q % 2
    twin = (p, z * 2 + 1 - core)
    block = core * 16 + z * 2
    feeder = 2 * ((p % NCOL) // 2) + p // NCOL

    def to_self(half):
        return (block + half == p) & (p % NCOL == q)

    def from_self(h):
        return (q + 16 * h == p) & (feeder == q)

    barrier = pltpu.get_barrier_semaphore()

    @pl.loop(1, 8)
    def _(d):
        pl.semaphore_signal(
            barrier, inc=1, device_id=(p, ((z + d) % 8) * 2 + core), device_id_type=MESH)

    pl.semaphore_signal(barrier, inc=1, device_id=twin, device_id_type=MESH)

    @pl.loop(1, NROW)
    def _(d):
        pl.semaphore_signal(barrier, inc=1, device_id=((p + d) % NROW, q), device_id_type=MESH)

    waits = 7 + 1 + NROW - 1
    for half in range(2):
        @pl.when(jnp.logical_not(to_self(half)))
        def _():
            pl.semaphore_signal(
                barrier, inc=1, device_id=(block + half, p % NCOL), device_id_type=MESH)

        @pl.when(jnp.logical_not(from_self(half)))
        def _():
            pl.semaphore_signal(
                barrier, inc=1, device_id=(q + 16 * half, feeder), device_id_type=MESH)

        waits += jnp.where(to_self(half), 0, 1) + jnp.where(from_self(half), 0, 1)

    head_in = pltpu.make_async_copy(x_ref.at[pl.ds(0, 256)], xv.at[pl.ds(0, 256)], xsem.at[0])
    rest_in = pltpu.make_async_copy(x_ref.at[pl.ds(256, 3840)], xv.at[pl.ds(256, 3840)], xsem.at[1])
    head_in.start()
    rest_in.start()
    head_in.wait()
    own[:, 0:HEAD] = xv[pl.ds(0, HEAD, stride=2), :].T[0:16, :]
    head[pl.ds(pl.multiple_of(z * 16, 16), 16), :] = own[:, 0:HEAD]
    rest_in.wait()

    @pl.loop(1, 16)
    def _(b):
        lanes = pl.ds(pl.multiple_of(b * 128, 128), 128)
        own[:, lanes] = xv[pl.ds(b * 256, 128, stride=2), :].T[0:16, :]

    pl.semaphore_wait(barrier, waits)

    def head_copy(d, origin):
        rows = pl.ds(pl.multiple_of(origin * 16, 16), 16)
        return pltpu.make_async_remote_copy(
            src_ref=own.at[:, pl.ds(0, HEAD)], dst_ref=head.at[rows, :], send_sem=hs.at[d],
            recv_sem=hr.at[d], device_id=(p, ((z + d) % 8) * 2 + core), device_id_type=MESH)

    @pl.loop(1, 8)
    def _(d):
        head_copy(d, z).start()

    side = pl.ds(pl.multiple_of((p // NCOL) * HEAD, HEAD), HEAD)

    def scatter_send(half):
        return pltpu.make_async_remote_copy(
            src_ref=own.at[pl.ds(half * 8, 8), pl.ds(0, HEAD)], dst_ref=b8.at[:, side],
            send_sem=ts.at[half], recv_sem=tr.at[p // NCOL],
            device_id=(block + half, p % NCOL), device_id_type=MESH)

    def scatter_recv(h):
        lanes = b8.at[:, pl.ds(h * HEAD, HEAD)]
        return pltpu.make_async_remote_copy(
            src_ref=lanes, dst_ref=lanes, send_sem=ts.at[0], recv_sem=tr.at[h],
            device_id=(block, p % NCOL), device_id_type=MESH)

    for half in range(2):
        @pl.when(jnp.logical_not(to_self(half)))
        def _():
            scatter_send(half).start()

        @pl.when(to_self(half))
        def _():
            b8[:, side] = own[half * 8:half * 8 + 8, 0:HEAD]

    def piece(dist, half, which):
        rows = which * 128 + ((z + 8 - dist) % 8) * 16
        start, size = HALF[half]
        return g_ref.at[pl.ds(pl.multiple_of(rows, 16), 16), pl.ds(start, size)]

    def source(dist, half):
        start, size = HALF[half]
        return own.at[:, pl.ds(start, size)] if dist == 0 else piece(dist, half, core)

    def ring_send(direction, step, half):
        dist = step - 1 if direction == 0 else (9 - step) % 8
        slot = step if direction == 0 else 8 - step
        to = (z + 1) % 8 if direction == 0 else (z + 7) % 8
        return pltpu.make_async_remote_copy(
            src_ref=source(dist, half), dst_ref=piece(dist, half, core),
            send_sem=rs.at[direction, half, step], recv_sem=rr.at[half, slot],
            device_id=(p, to * 2 + core), device_id_type=MESH)

    def ring_recv(direction, step, half):
        slot = step if direction == 0 else 8 - step
        return pltpu.make_async_remote_copy(
            src_ref=piece(slot, half, core), dst_ref=piece(slot, half, core),
            send_sem=rs.at[direction, half, step], recv_sem=rr.at[half, slot],
            device_id=twin, device_id_type=MESH)

    def twin_send(slot, half):
        return pltpu.make_async_remote_copy(
            src_ref=source(slot, half), dst_ref=piece(slot, half, core),
            send_sem=bs.at[half, slot], recv_sem=br.at[half, slot],
            device_id=twin, device_id_type=MESH)

    def twin_recv(slot, half):
        return pltpu.make_async_remote_copy(
            src_ref=piece(slot, half, 1 - core), dst_ref=piece(slot, half, 1 - core),
            send_sem=bs.at[half, slot], recv_sem=br.at[half, slot],
            device_id=twin, device_id_type=MESH)

    def ring_step(step):
        for half in range(2):
            for direction in range(2):
                last = REACH[direction, half]
                if step <= last:
                    ring_recv(direction, step, half).wait_recv()
                    if step < last:
                        ring_send(direction, step + 1, half).start()
                    twin_send(step if direction == 0 else 8 - step, half).start()

    for half in range(2):
        ring_send(0, 1, half).start()
        ring_send(1, 1, half).start()

    @pl.loop(1, 8)
    def _(d):
        head_copy(d, (z + 8 - d) % 8).wait_recv()

    g8[...] = head[...].T[0:8, :]
    mine = pl.ds(pl.multiple_of(p * 8, 8), 8)
    abuf[core, mine, :] = g8[...]

    def a_copy(d, origin):
        rows = pl.ds(pl.multiple_of(origin * 8, 8), 8)
        return pltpu.make_async_remote_copy(
            src_ref=g8, dst_ref=abuf.at[core, rows, :], send_sem=as_.at[d], recv_sem=ar.at[d],
            device_id=((p + d) % NROW, q), device_id_type=MESH)

    @pl.loop(1, NROW)
    def _(d):
        a_copy(d, p).start()

    for h in range(2):
        @pl.when(jnp.logical_not(from_self(h)))
        def _():
            scatter_recv(h).wait_recv()
    bbuf[mine, :] = b8[...]

    def b_copy(d, origin):
        rows = pl.ds(pl.multiple_of(origin * 8, 8), 8)
        return pltpu.make_async_remote_copy(
            src_ref=b8, dst_ref=bbuf.at[rows, :], send_sem=ks.at[d], recv_sem=kr.at[d],
            device_id=((p + d) % NROW, q), device_id_type=MESH)

    @pl.loop(1, NROW)
    def _(d):
        b_copy(d, p).start()

    def lead(which):
        return g_ref.at[pl.ds(pl.multiple_of(which * 128, 128), 128), pl.ds(0, HEAD)]

    lead_here = pltpu.make_async_copy(head, lead(core), osem.at[0])
    lead_here.start()
    own_rows = pl.ds(pl.multiple_of(core * 128 + z * 16, 16), 16)
    own_here = pltpu.make_async_copy(
        own.at[:, pl.ds(HEAD, ROWS - HEAD)], g_ref.at[own_rows, pl.ds(HEAD, ROWS - HEAD)],
        osem.at[1])
    own_here.start()

    def lead_there(which):
        return pltpu.make_async_remote_copy(
            src_ref=head, dst_ref=lead(which), send_sem=us.at[0], recv_sem=ur.at[0],
            device_id=twin, device_id_type=MESH)

    lead_there(core).start()
    for half in range(2):
        twin_send(0, half).start()

    ring_step(1)

    @pl.loop(1, NROW)
    def _(d):
        a_copy(d, (p + NROW - d) % NROW).wait_recv()

    def a_swap(which):
        return pltpu.make_async_remote_copy(
            src_ref=abuf.at[which], dst_ref=abuf.at[which], send_sem=us.at[1],
            recv_sem=ur.at[1], device_id=twin, device_id_type=MESH)

    a_swap(core).start()
    ring_step(2)
    a_swap(1 - core).wait_recv()

    row = lax.broadcasted_iota(jnp.int32, (256, 256), 0)
    col = lax.broadcasted_iota(jnp.int32, (256, 256), 1)
    row_order = one_hot(row == (col % 8) * NROW + col // 8)
    col_order = one_hot(col == (row % 16) * NCOL + ((row // 16) % 8) * 2 + row // 128)
    rows = pick_left(row_order, jnp.concatenate([abuf[0], abuf[1]], 1))
    sym[...] = jnp.where(
        row >= col, pick_right(rows, col_order), pick_left(col_order, rows, 0, 1))
    pick = one_hot(row[0:8] * NROW + p == col[0:8])
    h_ref[...] = pick_right(pick_left(pick, sym[...]), col_order, 1, 1)
    work[...] = sym[0:128, 0:128]

    @pl.loop(0, 2)
    def _(i):
        for k, v in enumerate(invert_factor([work[8 * k:8 * k + 8, :] for k in range(16)])):
            zd[i, 8 * k:8 * k + 8, :] = v

        @pl.when(i == 0)
        def _():
            low = mm(sym[128:256, 0:128], zd[0], 1, 1)
            work[...] = sym[128:256, 128:256] - mm(low, low, 1, 1)
            carry[...] = mm(low, zd[0])
            ring_step(3)

    ring_step(4)

    @pl.loop(1, NROW)
    def _(d):
        b_copy(d, (p + NROW - d) % NROW).wait_recv()

    zb[0:128, 0:128] = zd[0]
    zb[0:128, 128:256] = jnp.zeros((128, 128), jnp.float32)
    zb[128:256, 0:128] = -mm(zd[1], carry[...])
    zb[128:256, 128:256] = zd[1]
    inverse = pick_right(zb[...], col_order, 1, 1)
    cols = pick_right(bbuf[...], one_hot(col == (row % 128) * 2 + row // 128))
    own_cols = jnp.where(row == col * NCOL + q, 1.0, 0.0)
    t = jnp.where(col < 16, own_cols, mm(inverse, cols))
    w_ref[...] = mm(inverse, t, 0, 0)

    lead_there(1 - core).wait_recv()
    for half in range(2):
        for slot in range(8):
            twin_recv(slot, half).wait_recv()

    @pl.loop(1, 8)
    def _(d):
        head_copy(d, z).wait_send()

    @pl.loop(1, NROW)
    def _(d):
        a_copy(d, p).wait_send()
        b_copy(d, p).wait_send()

    for half in range(2):
        @pl.when(jnp.logical_not(to_self(half)))
        def _():
            scatter_send(half).wait_send()

    for half in range(2):
        for direction in range(2):
            for step in range(1, REACH[direction, half] + 1):
                ring_send(direction, step, half).wait_send()
        for slot in range(8):
            twin_send(slot, half).wait_send()
    lead_there(core).wait_send()
    a_swap(core).wait_send()
    lead_here.wait()
    own_here.wait()


def panel(x):
    dma = pltpu.SemaphoreType.DMA
    f32 = jnp.float32
    return pl.pallas_call(
        panel_kernel,
        out_shape=(
            jax.ShapeDtypeStruct((256, ROWS), f32),
            jax.ShapeDtypeStruct((256, 256), f32),
            jax.ShapeDtypeStruct((8, 256), f32),
        ),
        in_specs=[pl.BlockSpec(memory_space=pltpu.HBM)],
        out_specs=(
            pl.BlockSpec(memory_space=pltpu.HBM),
            pl.BlockSpec(memory_space=pltpu.VMEM),
            pl.BlockSpec(memory_space=pltpu.VMEM),
        ),
        scratch_shapes=[
            pltpu.VMEM((2 * ROWS, 128), f32),
            pltpu.VMEM((16, ROWS), f32),
            pltpu.VMEM((128, HEAD), f32),
            pltpu.VMEM((8, 128), f32),
            pltpu.VMEM((8, 256), f32),
            pltpu.VMEM((2, 256, 128), f32),
            pltpu.VMEM((256, 256), f32),
            pltpu.VMEM((256, 256), f32),
            pltpu.VMEM((128, 128), f32),
            pltpu.VMEM((128, 128), f32),
            pltpu.VMEM((2, 128, 128), f32),
            pltpu.VMEM((256, 256), f32),
            dma((2,)), dma((2,)),
            dma((8,)), dma((8,)),
            dma((2, 2, 5)), dma((2, 8)),
            dma((2, 8)), dma((2, 8)),
            dma((NROW,)), dma((NROW,)),
            dma((NROW,)), dma((NROW,)),
            dma((2,)), dma((2,)),
            dma((2,)), dma((2,)),
        ],
        compiler_params=pltpu.CompilerParams(
            collective_id=0, has_side_effects=True, vmem_limit_bytes=24 << 20),
        name="panel",
    )(pltpu.with_memory_space_constraint(x, pltpu.HBM))


def update_kernel(g_ref, w_ref, h_ref, x_ref, o_ref):
    p = lax.axis_index("row")
    q = lax.axis_index("col")
    size = g_ref.shape[1]
    first = pl.program_id(0) * size
    acc = lax.dot_general(
        g_ref[...], w_ref[...], (((0,), (0,)), ((), ())), precision=HIGH,
        preferred_element_type=jnp.float32)
    row = (first + lax.broadcasted_iota(jnp.int32, (size, 128), 0)) * NROW + p
    lane = lax.broadcasted_iota(jnp.int32, (size, 128), 1)
    left = jnp.where(lane < 16, acc[:, :128], x_ref[pl.ds(0, size, stride=2), :] - acc[:, :128])
    right = x_ref[pl.ds(1, size, stride=2), :] - acc[:, 128:]
    o_ref[pl.ds(0, size, stride=2), :] = jnp.where(row >= lane * NCOL + q, left, 0.0)
    o_ref[pl.ds(1, size, stride=2), :] = jnp.where(row >= (lane + 128) * NCOL + q, right, 0.0)

    @pl.when(pl.program_id(0) == 0)
    def _():
        keep = row[0:8] >= lane[0:8] * NCOL + q
        o_ref[pl.ds(0, 8, stride=2), :] = jnp.where(keep & (lane[0:8] < 16), mm(h_ref[...], w_ref[:, 0:128]), 0.0)


def update(g, w, h, x):
    size = 512
    return pl.pallas_call(
        update_kernel,
        grid=(ROWS // size,),
        out_shape=jax.ShapeDtypeStruct((2 * ROWS, 128), jnp.float32),
        in_specs=[
            pl.BlockSpec((256, size), lambda i: (0, i)),
            pl.BlockSpec((256, 256), lambda i: (0, 0)),
            pl.BlockSpec((8, 256), lambda i: (0, 0)),
            pl.BlockSpec((2 * size, 128), lambda i: (i, 0)),
        ],
        out_specs=pl.BlockSpec((2 * size, 128), lambda i: (i, 0)),
        compiler_params=pltpu.CompilerParams(vmem_limit_bytes=24 << 20),
        name="update",
    )(g, w, h, x)


def body(window):
    x = window.reshape(2 * ROWS, 128)
    g, w, h = panel(x)
    return update(g, w, h, x).reshape(1, ROWS, 1, COLS)


def solution(mesh):
    spec = P("row", None, "col", None)
    return jax.shard_map(body, mesh=mesh, in_specs=(spec,), out_specs=spec, check_vma=False)
```

time: 144 us -> 47.1 us (0.33)
  the two profiles are of different devices: /device:TPU:62 before, /device:TPU:1 now
where the time goes in v3:
time: 47.1 us; the launch traced here: 47 us
  Pallas kernels  47 us (100%)
    pallas_call x1, Pallas kernels, panel(): pl.pallas_call(panel_kernel, out_shape=(jax.ShapeDtypeStruct((256, ROWS),...  43.2 us
    pallas_call x1, Pallas kernels, update(): pl.pallas_call(update_kernel, grid=(ROWS // size,), out_shape=jax.ShapeDt...  3.78 us

profile of v3, /device:TPU:1, one launch (start us, length us, event | category | flops | bytes accessed | tf_op | source)
XLA Modules:
  0.0 47.0 jit_solution(9143153245338807752)
XLA Ops:
  0.0 0.0 copy-start
  0.0 43.2 %panel.1 = (f32[256,2048]{1,0:T(8,128)S(1)}, f32[256,256]{1,0:T(8,128)S(1)}, f32[8,256]{1,0:T(8,128)S(1)}) custom-call(f32[4096,128]{1,0:T(8,128)} %bitcast.2), custom_call_target="tpu_custom_call" | custom-call | tf_op jit(solution)/shard_map/panel/pallas_call | solution.py:382
  43.2 0.0 copy-done
  43.2 3.8 %update.1 = f32[4096,128]{1,0:T(8,128)} custom-call(f32[256,2048]{1,0:T(8,128)S(1)} %get-tuple-element.8.g_ref, f32[256,256]{1,0:T(8,128)S(1)} %get-tuple-element.9.w_ref, f32[8,256]{1,0:T(8,128)S(1)} %get-tuple-element.10.h_ref, f32[4096,128]{1,0:T(8,128)S(1)} %bitcast.3), custom_call_target="tpu_custom_call" | custom-call | tf_op jit(solution)/shard_map/update/pallas_call | solution.py:446
Async XLA Ops:
  0.0 43.2 %copy-start = (f32[1,2048,1,256]{3,2,1,0:T(1,128)S(1)}, f32[1,2048,1,256]{3,2,1,0:T(1,128)}, u32[]{:S(2)}) copy-start(f32[1,2048,1,256]{3,2,1,0:T(1,128)} %param.1) | copy-start | bytes 6291460

commit v4 on v3

--- a/solution.py
+++ b/solution.py
@@ -11,8 +11,10 @@
 ROWS = 2048
 COLS = 256
 HEAD = 128
+STRIP = 256
 HALF = ((128, 1024), (1152, 896))
 REACH = {(0, 0): 4, (1, 0): 3, (0, 1): 3, (1, 1): 4}
+SPOT = (12, 15)
 HIGH = lax.Precision.HIGHEST
 
 
@@ -25,12 +27,14 @@
 def sub_bcast(v, r):
     return jnp.broadcast_to(v[r:r+1, :], (8, 128))
 
-def invert_factor(m):
+def invert_factor(m, forward):
     lane = lax.broadcasted_iota(jnp.int32, (8, 128), 1)
     sub = lax.broadcasted_iota(jnp.int32, (8, 128), 0)
     m = list(m)
     out = []
     for j in range(16):
+        if j in SPOT:
+            forward(j)
         inside = (lane >= 8*j) & (lane < 8*j+8)
         own = [lane_bcast(m[j], 8*j+k) for k in range(8)]
         e = {(i, k): sub_bcast(own[k], i) for k in range(8) for i in range(k, 8)}
@@ -93,7 +97,7 @@
 
 def panel_kernel(
     x_ref, g_ref, w_ref, h_ref,
-    xv, own, head, g8, b8, abuf, bbuf, sym, work, carry, zd, zb,
+    xv, own, head, g8, b8, abuf, bbuf, sym, work, right, zd, inverse,
     xsem, osem, hs, hr, rs, rr, bs, br, as_, ar, ks, kr, ts, tr, us, ur,
 ):
     p = lax.axis_index("row")
@@ -144,47 +148,47 @@
     head_in.wait()
     own[:, 0:HEAD] = xv[pl.ds(0, HEAD, stride=2), :].T[0:16, :]
     head[pl.ds(pl.multiple_of(z * 16, 16), 16), :] = own[:, 0:HEAD]
+    pl.semaphore_wait(barrier, waits)
+
+    def head_copy(d, origin):
+        rows = pl.ds(pl.multiple_of(origin * 16, 16), 16)
+        return pltpu.make_async_remote_copy(
+            src_ref=own.at[:, pl.ds(0, HEAD)], dst_ref=head.at[rows, :], send_sem=hs.at[d],
+            recv_sem=hr.at[d], device_id=(p, ((z + d) % 8) * 2 + core), device_id_type=MESH)
+
+    @pl.loop(1, 8)
+    def _(d):
+        head_copy(d, z).start()
+
+    side = pl.ds(pl.multiple_of((p // NCOL) * HEAD, HEAD), HEAD)
+
+    def scatter_send(half):
+        return pltpu.make_async_remote_copy(
+            src_ref=own.at[pl.ds(half * 8, 8), pl.ds(0, HEAD)], dst_ref=b8.at[:, side],
+            send_sem=ts.at[half], recv_sem=tr.at[p // NCOL],
+            device_id=(block + half, p % NCOL), device_id_type=MESH)
+
+    def scatter_recv(h):
+        lanes = b8.at[:, pl.ds(h * HEAD, HEAD)]
+        return pltpu.make_async_remote_copy(
+            src_ref=lanes, dst_ref=lanes, send_sem=ts.at[0], recv_sem=tr.at[h],
+            device_id=(block, p % NCOL), device_id_type=MESH)
+
+    for half in range(2):
+        @pl.when(jnp.logical_not(to_self(half)))
+        def _():
+            scatter_send(half).start()
+
+        @pl.when(to_self(half))
+        def _():
+            b8[:, side] = own[half * 8:half * 8 + 8, 0:HEAD]
+
     rest_in.wait()
 
     @pl.loop(1, 16)
     def _(b):
         lanes = pl.ds(pl.multiple_of(b * 128, 128), 128)
         own[:, lanes] = xv[pl.ds(b * 256, 128, stride=2), :].T[0:16, :]
-
-    pl.semaphore_wait(barrier, waits)
-
-    def head_copy(d, origin):
-        rows = pl.ds(pl.multiple_of(origin * 16, 16), 16)
-        return pltpu.make_async_remote_copy(
-            src_ref=own.at[:, pl.ds(0, HEAD)], dst_ref=head.at[rows, :], send_sem=hs.at[d],
-            recv_sem=hr.at[d], device_id=(p, ((z + d) % 8) * 2 + core), device_id_type=MESH)
-
-    @pl.loop(1, 8)
-    def _(d):
-        head_copy(d, z).start()
-
-    side = pl.ds(pl.multiple_of((p // NCOL) * HEAD, HEAD), HEAD)
-
-    def scatter_send(half):
-        return pltpu.make_async_remote_copy(
-            src_ref=own.at[pl.ds(half * 8, 8), pl.ds(0, HEAD)], dst_ref=b8.at[:, side],
-            send_sem=ts.at[half], recv_sem=tr.at[p // NCOL],
-            device_id=(block + half, p % NCOL), device_id_type=MESH)
-
-    def scatter_recv(h):
-        lanes = b8.at[:, pl.ds(h * HEAD, HEAD)]
-        return pltpu.make_async_remote_copy(
-            src_ref=lanes, dst_ref=lanes, send_sem=ts.at[0], recv_sem=tr.at[h],
-            device_id=(block, p % NCOL), device_id_type=MESH)
-
-    for half in range(2):
-        @pl.when(jnp.logical_not(to_self(half)))
-        def _():
-            scatter_send(half).start()
-
-        @pl.when(to_self(half))
-        def _():
-            b8[:, side] = own[half * 8:half * 8 + 8, 0:HEAD]
 
     def piece(dist, half, which):
         rows = which * 128 + ((z + 8 - dist) % 8) * 16
@@ -245,16 +249,20 @@
     mine = pl.ds(pl.multiple_of(p * 8, 8), 8)
     abuf[core, mine, :] = g8[...]
 
+    def shifted(d, sign):
+        return ((p // 8 + 4 + sign * (d // 8)) % 4) * 8 + (p % 8 + 8 + sign * (d % 8)) % 8
+
     def a_copy(d, origin):
         rows = pl.ds(pl.multiple_of(origin * 8, 8), 8)
         return pltpu.make_async_remote_copy(
             src_ref=g8, dst_ref=abuf.at[core, rows, :], send_sem=as_.at[d], recv_sem=ar.at[d],
-            device_id=((p + d) % NROW, q), device_id_type=MESH)
+            device_id=(shifted(d, 1), q), device_id_type=MESH)
 
     @pl.loop(1, NROW)
     def _(d):
         a_copy(d, p).start()
 
+    ring_step(1)
     for h in range(2):
         @pl.when(jnp.logical_not(from_self(h)))
         def _():
@@ -265,11 +273,7 @@
         rows = pl.ds(pl.multiple_of(origin * 8, 8), 8)
         return pltpu.make_async_remote_copy(
             src_ref=b8, dst_ref=bbuf.at[rows, :], send_sem=ks.at[d], recv_sem=kr.at[d],
-            device_id=((p + d) % NROW, q), device_id_type=MESH)
-
-    @pl.loop(1, NROW)
-    def _(d):
-        b_copy(d, p).start()
+            device_id=(shifted(d, 1), q), device_id_type=MESH)
 
     def lead(which):
         return g_ref.at[pl.ds(pl.multiple_of(which * 128, 128), 128), pl.ds(0, HEAD)]
@@ -291,59 +295,74 @@
     for half in range(2):
         twin_send(0, half).start()
 
-    ring_step(1)
+
+    def a_swap(group, which):
+        rows = pl.ds(pl.multiple_of(((p // 8 + 4 - group) % 4) * 64, 64), 64)
+        return pltpu.make_async_remote_copy(
+            src_ref=abuf.at[which, rows, :], dst_ref=abuf.at[which, rows, :],
+            send_sem=us.at[1 + group], recv_sem=ur.at[1 + group], device_id=twin,
+            device_id_type=MESH)
+
+    for group in range(4):
+        @pl.loop(max(1, group * 8), group * 8 + 8)
+        def _(d):
+            a_copy(d, shifted(d, -1)).wait_recv()
+
+        a_swap(group, core).start()
+    ring_step(2)
 
     @pl.loop(1, NROW)
     def _(d):
-        a_copy(d, (p + NROW - d) % NROW).wait_recv()
-
-    def a_swap(which):
-        return pltpu.make_async_remote_copy(
-            src_ref=abuf.at[which], dst_ref=abuf.at[which], send_sem=us.at[1],
-            recv_sem=ur.at[1], device_id=twin, device_id_type=MESH)
-
-    a_swap(core).start()
-    ring_step(2)
-    a_swap(1 - core).wait_recv()
+        b_copy(d, p).start()
+
+    for group in range(4):
+        a_swap(group, 1 - core).wait_recv()
 
     row = lax.broadcasted_iota(jnp.int32, (256, 256), 0)
     col = lax.broadcasted_iota(jnp.int32, (256, 256), 1)
-    row_order = one_hot(row == (col % 8) * NROW + col // 8)
     col_order = one_hot(col == (row % 16) * NCOL + ((row // 16) % 8) * 2 + row // 128)
-    rows = pick_left(row_order, jnp.concatenate([abuf[0], abuf[1]], 1))
+    rows = jnp.concatenate([
+        jnp.concatenate([abuf[c, pl.ds(k, NROW, stride=8), :] for k in range(8)], 0)
+        for c in range(2)], 1)
     sym[...] = jnp.where(
         row >= col, pick_right(rows, col_order), pick_left(col_order, rows, 0, 1))
+    work[...] = sym[0:128, 0:128]
+
+    @pl.loop(0, 2)
+    def _(i):
+        def forward(j):
+            @pl.when((i == 0) & (j == SPOT[0]))
+            def _():
+                ring_step(3)
+
+            @pl.when((i == 1) & (j == SPOT[1]))
+            def _():
+                ring_step(4)
+
+        blocks = invert_factor([work[8 * k:8 * k + 8, :] for k in range(16)], forward)
+        for k, v in enumerate(blocks):
+            zd[8 * k:8 * k + 8, :] = v
+
+        @pl.when(i == 0)
+        def _():
+            low = mm(sym[128:256, 0:128], zd[...], 1, 1)
+            work[...] = sym[128:256, 128:256] - mm(low, low, 1, 1)
+            top = pick_right(zd[...], col_order[:, 0:128], 1, 1)
+            inverse[0:128, :] = top
+            right[...] = col_order[:, 128:256].astype(jnp.float32).T - mm(low, top)
+
+    @pl.loop(1, NROW)
+    def _(d):
+        b_copy(d, shifted(d, -1)).wait_recv()
+
+    inverse[128:256, :] = mm(zd[...], right[...])
+    cols = pick_right(bbuf[...], one_hot(col == (row % 128) * 2 + row // 128))
+    whole = pair(inverse[...])
+    own_cols = jnp.where(row == col * NCOL + q, 1.0, 0.0)
+    t = jnp.where(col < 16, own_cols, dot3(whole, pair(cols)))
+    w_ref[...] = dot3(whole, pair(t), 0, 0)
     pick = one_hot(row[0:8] * NROW + p == col[0:8])
     h_ref[...] = pick_right(pick_left(pick, sym[...]), col_order, 1, 1)
-    work[...] = sym[0:128, 0:128]
-
-    @pl.loop(0, 2)
-    def _(i):
-        for k, v in enumerate(invert_factor([work[8 * k:8 * k + 8, :] for k in range(16)])):
-            zd[i, 8 * k:8 * k + 8, :] = v
-
-        @pl.when(i == 0)
-        def _():
-            low = mm(sym[128:256, 0:128], zd[0], 1, 1)
-            work[...] = sym[128:256, 128:256] - mm(low, low, 1, 1)
-            carry[...] = mm(low, zd[0])
-            ring_step(3)
-
-    ring_step(4)
-
-    @pl.loop(1, NROW)
-    def _(d):
-        b_copy(d, (p + NROW - d) % NROW).wait_recv()
-
-    zb[0:128, 0:128] = zd[0]
-    zb[0:128, 128:256] = jnp.zeros((128, 128), jnp.float32)
-    zb[128:256, 0:128] = -mm(zd[1], carry[...])
-    zb[128:256, 128:256] = zd[1]
-    inverse = pick_right(zb[...], col_order, 1, 1)
-    cols = pick_right(bbuf[...], one_hot(col == (row % 128) * 2 + row // 128))
-    own_cols = jnp.where(row == col * NCOL + q, 1.0, 0.0)
-    t = jnp.where(col < 16, own_cols, mm(inverse, cols))
-    w_ref[...] = mm(inverse, t, 0, 0)
 
     lead_there(1 - core).wait_recv()
     for half in range(2):
@@ -371,7 +390,8 @@
         for slot in range(8):
             twin_send(slot, half).wait_send()
     lead_there(core).wait_send()
-    a_swap(core).wait_send()
+    for group in range(4):
+        a_swap(group, core).wait_send()
     lead_here.wait()
     own_here.wait()
 
@@ -402,8 +422,8 @@
             pltpu.VMEM((256, 256), f32),
             pltpu.VMEM((256, 256), f32),
             pltpu.VMEM((128, 128), f32),
+            pltpu.VMEM((128, 256), f32),
             pltpu.VMEM((128, 128), f32),
-            pltpu.VMEM((2, 128, 128), f32),
             pltpu.VMEM((256, 256), f32),
             dma((2,)), dma((2,)),
             dma((8,)), dma((8,)),
@@ -412,7 +432,7 @@
             dma((NROW,)), dma((NROW,)),
             dma((NROW,)), dma((NROW,)),
             dma((2,)), dma((2,)),
-            dma((2,)), dma((2,)),
+            dma((5,)), dma((5,)),
         ],
         compiler_params=pltpu.CompilerParams(
             collective_id=0, has_side_effects=True, vmem_limit_bytes=24 << 20),
@@ -420,40 +440,58 @@
     )(pltpu.with_memory_space_constraint(x, pltpu.HBM))
 
 
-def update_kernel(g_ref, w_ref, h_ref, x_ref, o_ref):
+def pair(v):
+    high = v.astype(jnp.bfloat16)
+    return high, (v - high.astype(jnp.float32)).astype(jnp.bfloat16)
+
+
+def dot3(a, b, ca=1, cb=0):
+    def one(u, v):
+        return lax.dot_general(
+            u, v, (((ca,), (cb,)), ((), ())), preferred_element_type=jnp.float32)
+
+    return one(a[0], b[0]) + (one(a[0], b[1]) + one(a[1], b[0]))
+
+
+def update_kernel(g_ref, w_ref, h_ref, x_ref, o_ref, ov, sem):
     p = lax.axis_index("row")
     q = lax.axis_index("col")
-    size = g_ref.shape[1]
-    first = pl.program_id(0) * size
-    acc = lax.dot_general(
-        g_ref[...], w_ref[...], (((0,), (0,)), ((), ())), precision=HIGH,
-        preferred_element_type=jnp.float32)
-    row = (first + lax.broadcasted_iota(jnp.int32, (size, 128), 0)) * NROW + p
-    lane = lax.broadcasted_iota(jnp.int32, (size, 128), 1)
-    left = jnp.where(lane < 16, acc[:, :128], x_ref[pl.ds(0, size, stride=2), :] - acc[:, :128])
-    right = x_ref[pl.ds(1, size, stride=2), :] - acc[:, 128:]
-    o_ref[pl.ds(0, size, stride=2), :] = jnp.where(row >= lane * NCOL + q, left, 0.0)
-    o_ref[pl.ds(1, size, stride=2), :] = jnp.where(row >= (lane + 128) * NCOL + q, right, 0.0)
-
-    @pl.when(pl.program_id(0) == 0)
-    def _():
-        keep = row[0:8] >= lane[0:8] * NCOL + q
-        o_ref[pl.ds(0, 8, stride=2), :] = jnp.where(keep & (lane[0:8] < 16), mm(h_ref[...], w_ref[:, 0:128]), 0.0)
+    size = STRIP
+    weights = pair(w_ref[...])
+    copies = []
+    for t in range(ROWS // size):
+        acc = dot3(pair(g_ref[:, t * size:(t + 1) * size]), weights, 0, 0)
+        start = 2 * t * size
+        row = (t * size + lax.broadcasted_iota(jnp.int32, (size, 128), 0)) * NROW + p
+        lane = lax.broadcasted_iota(jnp.int32, (size, 128), 1)
+        left = jnp.where(
+            lane < 16, acc[:, :128], x_ref[pl.ds(start, size, stride=2), :] - acc[:, :128])
+        right = x_ref[pl.ds(start + 1, size, stride=2), :] - acc[:, 128:]
+        if t * size * NROW < COLS * NCOL:
+            left = jnp.where(row >= lane * NCOL + q, left, 0.0)
+            right = jnp.where(row >= (lane + 128) * NCOL + q, right, 0.0)
+        ov[pl.ds(start, size, stride=2), :] = left
+        ov[pl.ds(start + 1, size, stride=2), :] = right
+        if t == 0:
+            keep = (row[0:8] >= lane[0:8] * NCOL + q) & (lane[0:8] < 16)
+            ov[pl.ds(0, 8, stride=2), :] = jnp.where(
+                keep, mm(h_ref[...], w_ref[:, 0:128]), 0.0)
+        copies.append(pltpu.make_async_copy(
+            ov.at[pl.ds(start, 2 * size)], o_ref.at[pl.ds(start, 2 * size)], sem.at[t]))
+        copies[-1].start()
+    for copy in copies:
+        copy.wait()
 
 
 def update(g, w, h, x):
-    size = 512
+    vmem = pl.BlockSpec(memory_space=pltpu.VMEM)
     return pl.pallas_call(
         update_kernel,
-        grid=(ROWS // size,),
         out_shape=jax.ShapeDtypeStruct((2 * ROWS, 128), jnp.float32),
-        in_specs=[
-            pl.BlockSpec((256, size), lambda i: (0, i)),
-            pl.BlockSpec((256, 256), lambda i: (0, 0)),
-            pl.BlockSpec((8, 256), lambda i: (0, 0)),
-            pl.BlockSpec((2 * size, 128), lambda i: (i, 0)),
-        ],
-        out_specs=pl.BlockSpec((2 * size, 128), lambda i: (i, 0)),
+        in_specs=[vmem, vmem, vmem, vmem],
+        out_specs=pl.BlockSpec(memory_space=pltpu.HBM),
+        scratch_shapes=[
+            pltpu.VMEM((2 * ROWS, 128), jnp.float32), pltpu.SemaphoreType.DMA((ROWS // STRIP,))],
         compiler_params=pltpu.CompilerParams(vmem_limit_bytes=24 << 20),
         name="update",
     )(g, w, h, x)

time: 47.1 us -> 43.7 us (0.928)
  Pallas kernels: 47 us -> 43.6 us
    pallas_call x1, Pallas kernels: 3.78 us -> 1.92 us  [update(): pl.pallas_call(update_kernel, out_shape=jax.ShapeDtypeStruct((2 * ROWS, 1...]
    pallas_call x1, Pallas kernels: 43.2 us -> 41.7 us  [panel(): pl.pallas_call(panel_kernel, out_shape=(jax.ShapeDtypeStruct((256, ROWS),...]
where the time goes in v4:
time: 43.7 us; the launch traced here: 43.6 us
  Pallas kernels  43.6 us (100%)
    pallas_call x1, Pallas kernels, panel(): pl.pallas_call(panel_kernel, out_shape=(jax.ShapeDtypeStruct((256, ROWS),...  41.7 us
    pallas_call x1, Pallas kernels, update(): pl.pallas_call(update_kernel, out_shape=jax.ShapeDtypeStruct((2 * ROWS, 1...  1.92 us

profile of v4, /device:TPU:1, one launch (start us, length us, event | category | flops | bytes accessed | tf_op | source)
XLA Modules:
  0.0 43.6 jit_solution(11567351381348766508)
XLA Ops:
  0.0 0.0 copy-start
  0.0 41.7 %panel.1 = (f32[256,2048]{1,0:T(8,128)S(1)}, f32[256,256]{1,0:T(8,128)S(1)}, f32[8,256]{1,0:T(8,128)S(1)}) custom-call(f32[4096,128]{1,0:T(8,128)} %bitcast.2), custom_call_target="tpu_custom_call" | custom-call | tf_op jit(solution)/shard_map/panel/pallas_call | solution.py:402
  41.7 0.0 copy-done
  41.7 1.9 %update.1 = f32[4096,128]{1,0:T(8,128)} custom-call(f32[256,2048]{1,0:T(8,128)S(1)} %get-tuple-element.8.g_ref, f32[256,256]{1,0:T(8,128)S(1)} %get-tuple-element.9.w_ref, f32[8,256]{1,0:T(8,128)S(1)} %get-tuple-element.10.h_ref, f32[4096,128]{1,0:T(8,128)S(1)} %bitcast.3), custom_call_target="tpu_custom_call" | custom-call | tf_op jit(solution)/shard_map/update/pallas_call | solution.py:488
Async XLA Ops:
  0.0 41.7 %copy-start = (f32[1,2048,1,256]{3,2,1,0:T(1,128)S(1)}, f32[1,2048,1,256]{3,2,1,0:T(1,128)}, u32[]{:S(2)}) copy-start(f32[1,2048,1,256]{3,2,1,0:T(1,128)} %param.1) | copy-start | bytes 6291460

commit v5 on v4

--- a/solution.py
+++ b/solution.py
@@ -97,7 +97,7 @@
 
 def panel_kernel(
     x_ref, g_ref, w_ref, h_ref,
-    xv, own, head, g8, b8, abuf, bbuf, sym, work, right, zd, inverse,
+    xv, own, head, g8, b8, abuf, bbuf, sym, work, right, zd, inverse, below, first, late_order,
     xsem, osem, hs, hr, rs, rr, bs, br, as_, ar, ks, kr, ts, tr, us, ur,
 ):
     p = lax.axis_index("row")
@@ -114,51 +114,54 @@
     def from_self(h):
         return (q + 16 * h == p) & (feeder == q)
 
-    barrier = pltpu.get_barrier_semaphore()
-
-    @pl.loop(1, 8)
-    def _(d):
-        pl.semaphore_signal(
-            barrier, inc=1, device_id=(p, ((z + d) % 8) * 2 + core), device_id_type=MESH)
-
-    pl.semaphore_signal(barrier, inc=1, device_id=twin, device_id_type=MESH)
-
-    @pl.loop(1, NROW)
-    def _(d):
-        pl.semaphore_signal(barrier, inc=1, device_id=((p + d) % NROW, q), device_id_type=MESH)
-
-    waits = 7 + 1 + NROW - 1
-    for half in range(2):
-        @pl.when(jnp.logical_not(to_self(half)))
-        def _():
-            pl.semaphore_signal(
-                barrier, inc=1, device_id=(block + half, p % NCOL), device_id_type=MESH)
-
-        @pl.when(jnp.logical_not(from_self(half)))
-        def _():
-            pl.semaphore_signal(
-                barrier, inc=1, device_id=(q + 16 * half, feeder), device_id_type=MESH)
-
-        waits += jnp.where(to_self(half), 0, 1) + jnp.where(from_self(half), 0, 1)
-
     head_in = pltpu.make_async_copy(x_ref.at[pl.ds(0, 256)], xv.at[pl.ds(0, 256)], xsem.at[0])
     rest_in = pltpu.make_async_copy(x_ref.at[pl.ds(256, 3840)], xv.at[pl.ds(256, 3840)], xsem.at[1])
     head_in.start()
     rest_in.start()
+
+    firsts = [lax.rem(p // 8 + i, 4) * 8 for i in range(4)]
+    seconds = [lax.rem(p % 8 + j, 8) for j in range(8)]
+    row_peers = [(firsts[d // 8] + seconds[d % 8], q) for d in range(1, NROW)]
+    z_peers = [(p, lax.rem(z + d, 8) * 2 + core) for d in range(1, 8)]
+
+    barrier = pltpu.get_barrier_semaphore()
+    for peer in z_peers + [twin] + row_peers:
+        pl.semaphore_signal(barrier, inc=1, device_id=peer, device_id_type=MESH)
+
+    waits = 7 + 1 + NROW - 1
+    for half in range(2):
+        @pl.when(jnp.logical_not(to_self(half)))
+        def _():
+            pl.semaphore_signal(
+                barrier, inc=1, device_id=(block + half, p % NCOL), device_id_type=MESH)
+
+        @pl.when(jnp.logical_not(from_self(half)))
+        def _():
+            pl.semaphore_signal(
+                barrier, inc=1, device_id=(q + 16 * half, feeder), device_id_type=MESH)
+
+        waits += jnp.where(to_self(half), 0, 1) + jnp.where(from_self(half), 0, 1)
+
     head_in.wait()
     own[:, 0:HEAD] = xv[pl.ds(0, HEAD, stride=2), :].T[0:16, :]
     head[pl.ds(pl.multiple_of(z * 16, 16), 16), :] = own[:, 0:HEAD]
     pl.semaphore_wait(barrier, waits)
 
-    def head_copy(d, origin):
-        rows = pl.ds(pl.multiple_of(origin * 16, 16), 16)
-        return pltpu.make_async_remote_copy(
-            src_ref=own.at[:, pl.ds(0, HEAD)], dst_ref=head.at[rows, :], send_sem=hs.at[d],
-            recv_sem=hr.at[d], device_id=(p, ((z + d) % 8) * 2 + core), device_id_type=MESH)
-
-    @pl.loop(1, 8)
-    def _(d):
-        head_copy(d, z).start()
+    z_rows = pl.ds(pl.multiple_of(z * 16, 16), 16)
+    head_sends = [
+        pltpu.make_async_remote_copy(
+            src_ref=own.at[:, pl.ds(0, HEAD)], dst_ref=head.at[z_rows, :], send_sem=hs.at[0],
+            recv_sem=hr.at[0], device_id=peer, device_id_type=MESH)
+        for peer in z_peers]
+    for copy in head_sends:
+        copy.start()
+
+    def bulk(ref, send_sem, recv_sem):
+        return pltpu.make_async_remote_copy(
+            src_ref=ref, dst_ref=ref, send_sem=send_sem, recv_sem=recv_sem, device_id=twin,
+            device_id_type=MESH)
+
+    heads = bulk(head.at[pl.ds(0, 112), :], hs.at[0], hr.at[0])
 
     side = pl.ds(pl.multiple_of((p // NCOL) * HEAD, HEAD), HEAD)
 
@@ -241,26 +244,16 @@
         ring_send(0, 1, half).start()
         ring_send(1, 1, half).start()
 
-    @pl.loop(1, 8)
-    def _(d):
-        head_copy(d, (z + 8 - d) % 8).wait_recv()
+    heads.wait_recv()
 
     g8[...] = head[...].T[0:8, :]
     mine = pl.ds(pl.multiple_of(p * 8, 8), 8)
     abuf[core, mine, :] = g8[...]
 
-    def shifted(d, sign):
-        return ((p // 8 + 4 + sign * (d // 8)) % 4) * 8 + (p % 8 + 8 + sign * (d % 8)) % 8
-
-    def a_copy(d, origin):
-        rows = pl.ds(pl.multiple_of(origin * 8, 8), 8)
-        return pltpu.make_async_remote_copy(
-            src_ref=g8, dst_ref=abuf.at[core, rows, :], send_sem=as_.at[d], recv_sem=ar.at[d],
-            device_id=(shifted(d, 1), q), device_id_type=MESH)
-
-    @pl.loop(1, NROW)
-    def _(d):
-        a_copy(d, p).start()
+    for d in range(1, NROW):
+        pltpu.make_async_remote_copy(
+            src_ref=g8, dst_ref=abuf.at[core, mine, :], send_sem=as_.at[0],
+            recv_sem=ar.at[d // 8], device_id=row_peers[d - 1], device_id_type=MESH).start()
 
     ring_step(1)
     for h in range(2):
@@ -268,12 +261,6 @@
         def _():
             scatter_recv(h).wait_recv()
     bbuf[mine, :] = b8[...]
-
-    def b_copy(d, origin):
-        rows = pl.ds(pl.multiple_of(origin * 8, 8), 8)
-        return pltpu.make_async_remote_copy(
-            src_ref=b8, dst_ref=bbuf.at[rows, :], send_sem=ks.at[d], recv_sem=kr.at[d],
-            device_id=(shifted(d, 1), q), device_id_type=MESH)
 
     def lead(which):
         return g_ref.at[pl.ds(pl.multiple_of(which * 128, 128), 128), pl.ds(0, HEAD)]
@@ -304,16 +291,16 @@
             device_id_type=MESH)
 
     for group in range(4):
-        @pl.loop(max(1, group * 8), group * 8 + 8)
-        def _(d):
-            a_copy(d, shifted(d, -1)).wait_recv()
-
+        count = 56 if group == 0 else 64
+        bulk(abuf.at[core, pl.ds(0, count), :], as_.at[0], ar.at[group]).wait_recv()
         a_swap(group, core).start()
     ring_step(2)
 
-    @pl.loop(1, NROW)
-    def _(d):
-        b_copy(d, p).start()
+    for peer in row_peers:
+        pltpu.make_async_remote_copy(
+            src_ref=b8, dst_ref=bbuf.at[mine, :], send_sem=ks.at[0], recv_sem=kr.at[0],
+            device_id=peer, device_id_type=MESH).start()
+    b_all = bulk(bbuf.at[pl.ds(0, 248), :], ks.at[0], kr.at[0])
 
     for group in range(4):
         a_swap(group, 1 - core).wait_recv()
@@ -327,9 +314,17 @@
     sym[...] = jnp.where(
         row >= col, pick_right(rows, col_order), pick_left(col_order, rows, 0, 1))
     work[...] = sym[0:128, 0:128]
+    late_order[...] = col_order[:, 128:256].astype(jnp.float32).T
+
+    below[...] = jnp.zeros((128, 128), jnp.float32)
+    first[...] = jnp.zeros((128, 128), jnp.float32)
 
     @pl.loop(0, 2)
     def _(i):
+        top = pick_right(first[...], col_order[:, 0:128], 1, 1)
+        inverse[0:128, :] = top
+        right[...] = late_order[...] - mm(below[...], top)
+
         def forward(j):
             @pl.when((i == 0) & (j == SPOT[0]))
             def _():
@@ -347,13 +342,10 @@
         def _():
             low = mm(sym[128:256, 0:128], zd[...], 1, 1)
             work[...] = sym[128:256, 128:256] - mm(low, low, 1, 1)
-            top = pick_right(zd[...], col_order[:, 0:128], 1, 1)
-            inverse[0:128, :] = top
-            right[...] = col_order[:, 128:256].astype(jnp.float32).T - mm(low, top)
-
-    @pl.loop(1, NROW)
-    def _(d):
-        b_copy(d, shifted(d, -1)).wait_recv()
+            below[...] = low
+            first[...] = zd[...]
+
+    b_all.wait_recv()
 
     inverse[128:256, :] = mm(zd[...], right[...])
     cols = pick_right(bbuf[...], one_hot(col == (row % 128) * 2 + row // 128))
@@ -369,14 +361,10 @@
         for slot in range(8):
             twin_recv(slot, half).wait_recv()
 
-    @pl.loop(1, 8)
-    def _(d):
-        head_copy(d, z).wait_send()
-
-    @pl.loop(1, NROW)
-    def _(d):
-        a_copy(d, p).wait_send()
-        b_copy(d, p).wait_send()
+    heads.wait_send()
+
+    bulk(abuf.at[core, pl.ds(0, 248), :], as_.at[0], ar.at[0]).wait_send()
+    b_all.wait_send()
 
     for half in range(2):
         @pl.when(jnp.logical_not(to_self(half)))
@@ -425,12 +413,15 @@
             pltpu.VMEM((128, 256), f32),
             pltpu.VMEM((128, 128), f32),
             pltpu.VMEM((256, 256), f32),
+            pltpu.VMEM((128, 128), f32),
+            pltpu.VMEM((128, 128), f32),
+            pltpu.VMEM((128, 256), f32),
             dma((2,)), dma((2,)),
-            dma((8,)), dma((8,)),
+            dma((1,)), dma((1,)),
             dma((2, 2, 5)), dma((2, 8)),
             dma((2, 8)), dma((2, 8)),
-            dma((NROW,)), dma((NROW,)),
-            dma((NROW,)), dma((NROW,)),
+            dma((1,)), dma((4,)),
+            dma((1,)), dma((1,)),
             dma((2,)), dma((2,)),
             dma((5,)), dma((5,)),
         ],

time: 43.7 us -> 42 us (0.961)
  Pallas kernels: 43.6 us -> 41.8 us
    pallas_call x1, Pallas kernels: 41.7 us -> 39.9 us  [panel(): pl.pallas_call(panel_kernel, out_shape=(jax.ShapeDtypeStruct((256, ROWS),...]
where the time goes in v5:
time: 42 us; the launch traced here: 41.9 us
  Pallas kernels  41.8 us (100%)
    pallas_call x1, Pallas kernels, panel(): pl.pallas_call(panel_kernel, out_shape=(jax.ShapeDtypeStruct((256, ROWS),...  39.9 us
    pallas_call x1, Pallas kernels, update(): pl.pallas_call(update_kernel, out_shape=jax.ShapeDtypeStruct((2 * ROWS, 1...  1.92 us

profile of v5, /device:TPU:1, one launch (start us, length us, event | category | flops | bytes accessed | tf_op | source)
XLA Modules:
  0.0 41.9 jit_solution(9804242135278107879)
XLA Ops:
  0.0 0.0 copy-start
  0.0 39.9 %panel.1 = (f32[256,2048]{1,0:T(8,128)S(1)}, f32[256,256]{1,0:T(8,128)S(1)}, f32[8,256]{1,0:T(8,128)S(1)}) custom-call(f32[4096,128]{1,0:T(8,128)} %bitcast.2), custom_call_target="tpu_custom_call" | custom-call | tf_op jit(solution)/shard_map/panel/pallas_call | solution.py:390
  39.9 0.0 copy-done
  39.9 1.9 %update.1 = f32[4096,128]{1,0:T(8,128)} custom-call(f32[256,2048]{1,0:T(8,128)S(1)} %get-tuple-element.8.g_ref, f32[256,256]{1,0:T(8,128)S(1)} %get-tuple-element.9.w_ref, f32[8,256]{1,0:T(8,128)S(1)} %get-tuple-element.10.h_ref, f32[4096,128]{1,0:T(8,128)S(1)} %bitcast.3), custom_call_target="tpu_custom_call" | custom-call | tf_op jit(solution)/shard_map/update/pallas_call | solution.py:479
Async XLA Ops:
  0.0 39.9 %copy-start = (f32[1,2048,1,256]{3,2,1,0:T(1,128)S(1)}, f32[1,2048,1,256]{3,2,1,0:T(1,128)}, u32[]{:S(2)}) copy-start(f32[1,2048,1,256]{3,2,1,0:T(1,128)} %param.1) | copy-start | bytes 6291460

commit v6 on v5

--- a/solution.py
+++ b/solution.py
@@ -13,6 +13,8 @@
 HEAD = 128
 STRIP = 256
 HALF = ((128, 1024), (1152, 896))
+FIRST_ORDER = (2, 1, 3, 0)
+SECOND_ORDER = (4, 3, 5, 2, 6, 1, 7, 0)
 REACH = {(0, 0): 4, (1, 0): 3, (0, 1): 3, (1, 1): 4}
 SPOT = (12, 15)
 HIGH = lax.Precision.HIGHEST
@@ -121,8 +123,9 @@
 
     firsts = [lax.rem(p // 8 + i, 4) * 8 for i in range(4)]
     seconds = [lax.rem(p % 8 + j, 8) for j in range(8)]
-    row_peers = [(firsts[d // 8] + seconds[d % 8], q) for d in range(1, NROW)]
-    z_peers = [(p, lax.rem(z + d, 8) * 2 + core) for d in range(1, 8)]
+    steps = [(i, j) for i in FIRST_ORDER for j in SECOND_ORDER if i + j > 0]
+    row_peers = [(firsts[i] + seconds[j], q) for i, j in steps]
+    z_peers = [(p, lax.rem(z + j, 8) * 2 + core) for j in SECOND_ORDER if j > 0]
 
     barrier = pltpu.get_barrier_semaphore()
     for peer in z_peers + [twin] + row_peers:
@@ -250,10 +253,10 @@
     mine = pl.ds(pl.multiple_of(p * 8, 8), 8)
     abuf[core, mine, :] = g8[...]
 
-    for d in range(1, NROW):
+    for (i, _), peer in zip(steps, row_peers):
         pltpu.make_async_remote_copy(
             src_ref=g8, dst_ref=abuf.at[core, mine, :], send_sem=as_.at[0],
-            recv_sem=ar.at[d // 8], device_id=row_peers[d - 1], device_id_type=MESH).start()
+            recv_sem=ar.at[i], device_id=peer, device_id_type=MESH).start()
 
     ring_step(1)
     for h in range(2):
@@ -290,7 +293,7 @@
             send_sem=us.at[1 + group], recv_sem=ur.at[1 + group], device_id=twin,
             device_id_type=MESH)
 
-    for group in range(4):
+    for group in FIRST_ORDER:
         count = 56 if group == 0 else 64
         bulk(abuf.at[core, pl.ds(0, count), :], as_.at[0], ar.at[group]).wait_recv()
         a_swap(group, core).start()

time: 42 us -> 41 us (0.976)
  Pallas kernels: 41.8 us -> 40.9 us
    pallas_call x1, Pallas kernels: 39.9 us -> 38.9 us  [panel(): pl.pallas_call(panel_kernel, out_shape=(jax.ShapeDtypeStruct((256, ROWS),...]
where the time goes in v6:
time: 41 us; the launch traced here: 40.9 us
  Pallas kernels  40.9 us (100%)
    pallas_call x1, Pallas kernels, panel(): pl.pallas_call(panel_kernel, out_shape=(jax.ShapeDtypeStruct((256, ROWS),...  38.9 us
    pallas_call x1, Pallas kernels, update(): pl.pallas_call(update_kernel, out_shape=jax.ShapeDtypeStruct((2 * ROWS, 1...  1.92 us

profile of v6, /device:TPU:1, one launch (start us, length us, event | category | flops | bytes accessed | tf_op | source)
XLA Modules:
  0.0 40.9 jit_solution(12673712471807924702)
XLA Ops:
  0.0 0.0 copy-start
  0.0 38.9 %panel.1 = (f32[256,2048]{1,0:T(8,128)S(1)}, f32[256,256]{1,0:T(8,128)S(1)}, f32[8,256]{1,0:T(8,128)S(1)}) custom-call(f32[4096,128]{1,0:T(8,128)} %bitcast.2), custom_call_target="tpu_custom_call" | custom-call | tf_op jit(solution)/shard_map/panel/pallas_call | solution.py:393
  38.9 0.0 copy-done
  39.0 1.9 %update.1 = f32[4096,128]{1,0:T(8,128)} custom-call(f32[256,2048]{1,0:T(8,128)S(1)} %get-tuple-element.8.g_ref, f32[256,256]{1,0:T(8,128)S(1)} %get-tuple-element.9.w_ref, f32[8,256]{1,0:T(8,128)S(1)} %get-tuple-element.10.h_ref, f32[4096,128]{1,0:T(8,128)S(1)} %bitcast.3), custom_call_target="tpu_custom_call" | custom-call | tf_op jit(solution)/shard_map/update/pallas_call | solution.py:482
Async XLA Ops:
  0.0 39.0 %copy-start = (f32[1,2048,1,256]{3,2,1,0:T(1,128)S(1)}, f32[1,2048,1,256]{3,2,1,0:T(1,128)}, u32[]{:S(2)}) copy-start(f32[1,2048,1,256]{3,2,1,0:T(1,128)} %param.1) | copy-start | bytes 6291460

commit v7 on v6

--- a/solution.py
+++ b/solution.py
@@ -16,7 +16,7 @@
 FIRST_ORDER = (2, 1, 3, 0)
 SECOND_ORDER = (4, 3, 5, 2, 6, 1, 7, 0)
 REACH = {(0, 0): 4, (1, 0): 3, (0, 1): 3, (1, 1): 4}
-SPOT = (12, 15)
+SPOT = (11, 10)
 HIGH = lax.Precision.HIGHEST
 
 
@@ -128,7 +128,7 @@
     z_peers = [(p, lax.rem(z + j, 8) * 2 + core) for j in SECOND_ORDER if j > 0]
 
     barrier = pltpu.get_barrier_semaphore()
-    for peer in z_peers + [twin] + row_peers:
+    for peer in z_peers + [twin]:
         pl.semaphore_signal(barrier, inc=1, device_id=peer, device_id_type=MESH)
 
     waits = 7 + 1 + NROW - 1
@@ -144,6 +144,9 @@
                 barrier, inc=1, device_id=(q + 16 * half, feeder), device_id_type=MESH)
 
         waits += jnp.where(to_self(half), 0, 1) + jnp.where(from_self(half), 0, 1)
+
+    for peer in row_peers:
+        pl.semaphore_signal(barrier, inc=1, device_id=peer, device_id_type=MESH)
 
     head_in.wait()
     own[:, 0:HEAD] = xv[pl.ds(0, HEAD, stride=2), :].T[0:16, :]

time: 41 us -> 40.7 us (level)
  no operation moved by 1% of the time
where the time goes in v7:
time: 40.7 us; the launch traced here: 40.6 us
  Pallas kernels  40.5 us (100%)
    pallas_call x1, Pallas kernels, panel(): pl.pallas_call(panel_kernel, out_shape=(jax.ShapeDtypeStruct((256, ROWS),...  38.6 us
    pallas_call x1, Pallas kernels, update(): pl.pallas_call(update_kernel, out_shape=jax.ShapeDtypeStruct((2 * ROWS, 1...  1.92 us

profile of v7, /device:TPU:1, one launch (start us, length us, event | category | flops | bytes accessed | tf_op | source)
XLA Modules:
  0.0 40.6 jit_solution(5361733481766722806)
XLA Ops:
  0.0 0.0 copy-start
  0.0 38.6 %panel.1 = (f32[256,2048]{1,0:T(8,128)S(1)}, f32[256,256]{1,0:T(8,128)S(1)}, f32[8,256]{1,0:T(8,128)S(1)}) custom-call(f32[4096,128]{1,0:T(8,128)} %bitcast.2), custom_call_target="tpu_custom_call" | custom-call | tf_op jit(solution)/shard_map/panel/pallas_call | solution.py:396
  38.6 0.0 copy-done
  38.7 1.9 %update.1 = f32[4096,128]{1,0:T(8,128)} custom-call(f32[256,2048]{1,0:T(8,128)S(1)} %get-tuple-element.8.g_ref, f32[256,256]{1,0:T(8,128)S(1)} %get-tuple-element.9.w_ref, f32[8,256]{1,0:T(8,128)S(1)} %get-tuple-element.10.h_ref, f32[4096,128]{1,0:T(8,128)S(1)} %bitcast.3), custom_call_target="tpu_custom_call" | custom-call | tf_op jit(solution)/shard_map/update/pallas_call | solution.py:485
Async XLA Ops:
  0.0 38.6 %copy-start = (f32[1,2048,1,256]{3,2,1,0:T(1,128)S(1)}, f32[1,2048,1,256]{3,2,1,0:T(1,128)}, u32[]{:S(2)}) copy-start(f32[1,2048,1,256]{3,2,1,0:T(1,128)} %param.1) | copy-start | bytes 6291460
